TPU v7x, 768 devices: a whole 4x8x12 slice. The times are simulated.
768 devices in a mesh: dp: 48 (over z, y_hi), mp: 8 (over y_lo, x), phase: 2 (over core).
Axes of the slice: x: 4, y: 8 (y_hi: 4, y_lo: 2; y = y_hi * 2 + y_lo), z: 12, core: 2. Of those that a mesh axis runs over, the one named last changes fastest.
Arguments:
- item_owner: int32 [24576, 1], P('dp'), may hold values from 0 to 47; in each aligned block of 512 rows (0 to 511, 512 to 1023, ...) at most 18 rows name the same one
- item_row: int32 [24576], P('dp'), may hold values from 0 to 1023
- segments: int32 [48, 2, 256], P('dp'), may hold values from 0 to 31, never falling along the last dimension, each value on 1 to 128 neighbouring positions
- neighbors: int32 [48, 2, 256, 8], P('dp'), may hold values from 0 to 255
- table: bfloat16 [49152, 1024], P('dp'), may hold values from -6 to 6
- gains: bfloat16 [2, 1024], P('phase'), may hold values from 0.099609375 to 1.8984375
- w_in: bfloat16 [2, 1024, 4, 1024], P('phase', None, None, 'mp'), may hold values from -0.1875 to 0.1875
- w_out: bfloat16 [2, 1024, 1024], P('phase', 'mp'), may hold values from -0.1875 to 0.1875
- w_ctx: bfloat16 [1024, 1024], P(None, 'mp'), may hold values from -0.1875 to 0.1875
- ctx_bias: bfloat16 [1024], P('mp'), may hold values from -3 to 3
Outputs:
- user_states: bfloat16 [48, 2, 256, 1024], P('dp', 'phase')
- impression_context: bfloat16 [48, 2, 256, 1024], P('dp', 'phase', None, 'mp')
Inputs may be any that keep to these rules, and one draw needn't show every extreme that they name: `item_owner`: among the rows of one index of dp, at most 18 name the same owner.
All inputs are finite; a program needn't handle non-finite values.
Results may differ from a plain program's by a relative error of at most 0.02.
Values may be sent and summed in bfloat16 or wider, within the bound.
A program may use at most 32 MiB of HBM per device.

v0:
```python
import jax
import jax.numpy as jnp
from jax import lax
from jax.sharding import PartitionSpec as P

HD = 128
NBR = 8
MB_ROWS = 256


norm_eps = 1e-06


def passed_along(block, axis, distance):
    devices = range(lax.axis_size(axis))
    route = [((i - distance) % len(devices), i) for i in devices]
    return lax.ppermute(block, axis, route)


def hstu_local(acts, seg_ids, gain, w_proj, w_back):
    rows_n = acts.shape[0]
    width = acts.shape[1]
    local_cols = w_back.shape[0]
    local_heads = local_cols // HD
    acts_f = acts.astype(jnp.float32)
    inv_rms = lax.rsqrt(jnp.mean(acts_f * acts_f, axis=-1, keepdims=True) + norm_eps)
    normed = (acts_f * inv_rms * gain.astype(jnp.float32)).astype(jnp.bfloat16)
    projected = jnp.dot(
        normed, w_proj.reshape(width, 4 * local_cols), preferred_element_type=jnp.float32
    )
    projected = jax.nn.silu(projected).astype(jnp.bfloat16).reshape(rows_n, 4, local_heads, HD)
    gates_u = projected[:, 0]
    values_h = projected[:, 1]
    queries = projected[:, 2]
    keys_h = projected[:, 3]
    scores = jnp.einsum(
        "qhd,khd->hqk", queries, keys_h, preferred_element_type=jnp.float32
    ) * HD ** (-0.5)
    position = jnp.arange(rows_n)
    allowed = (position[None, :] <= position[:, None]) & (seg_ids[:, None] == seg_ids[None, :])
    weights = (jnp.where(allowed[None], jax.nn.silu(scores), 0.0) / MB_ROWS).astype(jnp.bfloat16)
    mixed = jnp.einsum("hqk,khd->qhd", weights, values_h, preferred_element_type=jnp.float32)
    mixed = mixed * lax.rsqrt(jnp.mean(mixed * mixed, axis=-1, keepdims=True) + norm_eps)
    gated = (mixed * gates_u.astype(jnp.float32)).astype(jnp.bfloat16).reshape(rows_n, local_cols)
    partial_term = jnp.dot(gated, w_back, preferred_element_type=jnp.float32)
    summed = lax.psum(partial_term.astype(jnp.bfloat16), "mp").astype(jnp.float32)
    return (acts_f + summed).astype(jnp.bfloat16)


def context_local(states, neigh_rows, w_ctx, ctx_bias):
    picked = jnp.take(states, neigh_rows.reshape(-1), axis=0).astype(jnp.float32)
    context = jnp.mean(picked.reshape(neigh_rows.shape[0], NBR, states.shape[1]), axis=1).astype(
        jnp.bfloat16
    )
    summed = jnp.dot(context, w_ctx, preferred_element_type=jnp.float32) + ctx_bias.astype(
        jnp.float32
    )
    return jax.nn.silu(summed).astype(jnp.bfloat16)


def on_device(
    item_owner, item_row, segments, neighbors, table, gains, w_in, w_out, w_ctx, ctx_bias
):
    dp_count = lax.axis_size("dp")
    row_total = item_row.shape[0]
    capacity = max(2, 7 * row_total // (4 * dp_count))
    owners = item_owner[:, 0]
    owner_hits = (owners[:, None] == jnp.arange(dp_count, dtype=jnp.int32)[None, :]).astype(
        jnp.int32
    )
    slot_rank = jnp.sum((jnp.cumsum(owner_hits, axis=0) - 1) * owner_hits, axis=1)
    slot_index = owners * capacity + slot_rank
    requests = jnp.full((dp_count * capacity,), -1, jnp.int32).at[slot_index].set(item_row)
    requests = requests.reshape(dp_count, capacity)
    found = jnp.take(
        table,
        jnp.maximum(lax.all_to_all(requests, "dp", split_axis=0, concat_axis=0, tiled=True), 0),
        axis=0,
    )
    fetched = lax.all_to_all(found, "dp", split_axis=0, concat_axis=0, tiled=True)
    width = table.shape[1]
    batches = segments.shape[1]
    acts_all = fetched.reshape(dp_count * capacity, width)[slot_index].reshape(batches, -1, width)
    batch_rows = acts_all.shape[1]
    impressions = neighbors.shape[2]
    ctx_cols = w_ctx.shape[1]
    phase_index = lax.axis_index("phase")
    is_first = phase_index == 0
    w_proj = w_in[0]
    w_back = w_out[0]
    gain = gains[0]
    empty_ctx = jnp.zeros((impressions, ctx_cols), jnp.bfloat16)
    recv_states = jnp.zeros((batch_rows, width), jnp.bfloat16)
    back_states = recv_states
    back_ctx = empty_ctx
    final_states = recv_states
    final_ctx = empty_ctx
    for round_index in range(batches + 1):
        micro_index = jnp.clip(round_index - phase_index, 0, batches - 1)
        seg_ids = lax.dynamic_index_in_dim(segments[0], micro_index, 0, keepdims=False)
        neigh_rows = lax.dynamic_index_in_dim(neighbors[0], micro_index, 0, keepdims=False)
        layer_input = jnp.where(is_first, acts_all[min(round_index, batches - 1)], recv_states)
        layer_out = hstu_local(layer_input, seg_ids, gain, w_proj, w_back)
        scored = lax.cond(
            is_first,
            lambda: empty_ctx,
            lambda: context_local(layer_out, neigh_rows, w_ctx, ctx_bias),
        )
        if round_index == batches:
            final_states = layer_out
            final_ctx = scored
        else:
            recv_states, recv_ctx = passed_along((layer_out, scored), "phase", 1)
            if round_index == batches - 1:
                back_states = recv_states
                back_ctx = recv_ctx
    user_states = jnp.where(is_first, back_states, final_states)
    impression_context = jnp.where(is_first, back_ctx, final_ctx)
    return (
        user_states.reshape(1, 1, batch_rows, width),
        impression_context.reshape(1, 1, impressions, ctx_cols),
    )


def solution(mesh):
    in_specs = (
        P("dp", None),
        P("dp"),
        P("dp", None, None),
        P("dp", None, None, None),
        P("dp", None),
        P("phase", None),
        P("phase", None, None, "mp"),
        P("phase", "mp", None),
        P(None, "mp"),
        P("mp"),
    )
    out_specs = (P("dp", "phase", None, None), P("dp", "phase", None, "mp"))
    return jax.shard_map(
        on_device, mesh=mesh, in_specs=in_specs, out_specs=out_specs, check_vma=False
    )
```

profile of v0, /device:TPU:1, one launch (start us, length us, event | category | flops | bytes accessed | tf_op | source)
XLA Modules:
  0.0 483.0 jit_solution(13717777877124504630)
XLA Ops:
  11.0 2.6 scatter_custom_fusion
  13.7 34.8 %all_to_all.14 = s32[48,1,18]{2,1,0:T(1,128)S(1)} all-to-all(s32[48,1,18]{2,1,0:T(1,128)S(1)} %bitcast.165), channel_id=1, replica_groups=mesh['dp'=48,'mp'=8,'phase'=2] {'dp'}, dimensions={0} | all-to-all | bytes 6912 | tf_op jit(solution)/shard_map/all_to_all | solution.py:77
  48.8 4.2 gather_fusion.2
  53.0 3.8 reshape.367
  56.9 3.3 broadcast_select_fusion
  60.2 5.6 %all-to-all-start.1 = ((bf16[48,18,1024]{2,1,0:T(8,128)(2,1)}), bf16[48,18,1024]{2,1,0:T(8,128)(2,1)}, u32[]{:S(2)}, u32[]{:S(2)}) async-start(bf16[48,18,1024]{2,1,0:T(8,128)(2,1)} %broadcast_select_fusion), calls=%async_computation.1 | async-start | bytes 4718592 | tf_op jit(solution)/shard_map/all_to_all | solution.py:80
  66.5 80.0 %all-to-all-done.1 = bf16[48,18,1024]{2,1,0:T(8,128)(2,1)} async-done(((bf16[48,18,1024]{2,1,0:T(8,128)(2,1)}), bf16[48,18,1024]{2,1,0:T(8,128)(2,1)}, u32[]{:S(2)}, u32[]{:S(2)}) %all-to-all-start.1) | async-done | bytes 1769504 | tf_op jit(solution)/shard_map/all_to_all | solution.py:80
  146.5 3.9 reshape.324
  150.4 4.4 gather_fusion.3
  155.1 2.6 multiply_convert_fusion.12
  157.7 1.8 reshape.325
  159.5 2.6 fusion.115
  162.0 2.1 multiply_reduce_fusion.2
  164.9 2.0 convolution_convert_fusion.2
  167.0 85.8 %all-reduce.4.cloned.1.call-done = bf16[256,1024]{1,0:T(8,128)(2,1)} async-done(((bf16[256,1024]{1,0:T(8,128)(2,1)}), bf16[256,1024]{1,0:T(8,128)(2,1)}) %all-reduce.4.cloned.1.call-update) | async-done | bytes 524304 | tf_op jit(solution)/shard_map/psum | solution.py:46
  252.7 1.3 fusion.9
  254.1 7.5 %collective-permute-start = (bf16[256,1024]{1,0:T(8,128)(2,1)S(1)}, bf16[256,1024]{1,0:T(8,128)(2,1)S(1)}, u32[]{:S(2)}, u32[]{:S(2)}) collective-permute-start(bf16[256,1024]{1,0:T(8,128)(2,1)S(1)} %fusion.9), channel_id=1, source_target_pairs={{1,0},{0,1},{3,2},{2,3},{5,4},{4,5},{7,6},{6,7},{9,8},{8,9},{11,10... | collective-permute-start | bytes 1572872 | tf_op jit(solution)/shard_map/ppermute | solution.py:17
  261.6 1.5 collective-permute-done
  268.6 85.8 %all-reduce.6.cloned.1.call-done = bf16[256,1024]{1,0:T(8,128)(2,1)} async-done(((bf16[256,1024]{1,0:T(8,128)(2,1)}), bf16[256,1024]{1,0:T(8,128)(2,1)}) %all-reduce.6.cloned.1.call-update) | async-done | bytes 524304 | tf_op jit(solution)/shard_map/psum | solution.py:46
  355.7 7.7 %collective-permute-start.1 = (bf16[256,1024]{1,0:T(8,128)(2,1)S(1)}, bf16[256,1024]{1,0:T(8,128)(2,1)S(1)}, u32[]{:S(2)}, u32[]{:S(2)}) collective-permute-start(bf16[256,1024]{1,0:T(8,128)(2,1)S(1)} %fusion.13), channel_id=1, source_target_pairs={{1,0},{0,1},{3,2},{2,3},{5,4},{4,5},{7,6},{6,7},{9,8},{8,9},{11,10... | collective-permute-start | bytes 1572872 | tf_op jit(solution)/shard_map/ppermute | solution.py:17
  363.4 1.3 collective-permute-done.1
  364.8 1.5 fusion.14
  370.4 1.3 multiply_reduce_fusion
  373.0 14.7 %conditional.2 = (bf16[256,128]{1,0:T(8,128)(2,1)S(1)}) conditional(s32[]{:T(128)} %convert_element_type.191, (s32[1,2,256,8]{2,3,1,0:T(8,128)S(1)}, s32[]{:T(128)}, bf16[256,1024]{1,0:T(8,128)(2,1)S(1)}, bf16[1024,128]{1,0:T(8,128)(2,1)}, bf16[128]{0:T(256)(128)(2,1)}) %tuple.64, () %tuple.26), branch_computations={%region_13.16_spmd, %region_15.17_spmd} | conditional | flops 73879680 | bytes 16161092 | solution.py:104
  373.3 9.7 %gather_fusion = bf16[2048,1024]{1,0:T(8,128)(2,1)} fusion(bf16[256,1024]{1,0:T(8,128)(2,1)S(1)} %get-tuple-element.53, s32[2048]{0:T(1024)S(1)} %fusion.1), kind=kCustom, calls=%fused_computation.clone | custom fusion | bytes 8396800 | tf_op jit(solution)/shard_map/cond/branch_0_fun/jit(_take)/gather | solution.py:51
  383.0 4.4 convert_reduce_fusion
  387.8 2.1 collective-permute-start.2
  389.8 69.1 %all-reduce.8.cloned.1.call-done = bf16[256,1024]{1,0:T(8,128)(2,1)} async-done(((bf16[256,1024]{1,0:T(8,128)(2,1)}), bf16[256,1024]{1,0:T(8,128)(2,1)}) %all-reduce.8.cloned.1.call-update) | async-done | bytes 524304 | tf_op jit(solution)/shard_map/psum | solution.py:46
  458.9 2.3 select_bitcast_fusion
  461.2 14.6 %conditional.3 = (bf16[256,128]{1,0:T(8,128)(2,1)S(1)}) conditional(s32[]{:T(128)} %convert_element_type.191, (s32[1,2,256,8]{2,3,1,0:T(8,128)S(1)}, s32[]{:T(128)}, bf16[256,1024]{1,0:T(8,128)(2,1)S(1)}, bf16[1024,128]{1,0:T(8,128)(2,1)S(1)}, bf16[128]{0:T(256)(128)(2,1)}) %tuple.65, () %tuple.28), branch_computations={%region_16.19_spmd, %region_18.20_spmd} | conditional | flops 73879680 | bytes 15112488 | solution.py:104
  461.5 9.7 %gather_fusion.1 = bf16[2048,1024]{1,0:T(8,128)(2,1)} fusion(bf16[256,1024]{1,0:T(8,128)(2,1)S(1)} %get-tuple-element.58, s32[2048]{0:T(1024)S(1)} %fusion.4), kind=kCustom, calls=%fused_computation.1.clone | custom fusion | bytes 8396800 | tf_op jit(solution)/shard_map/cond/branch_0_fun/jit(_take)/gather | solution.py:51
  471.2 4.3 convert_reduce_fusion.1
  (95 shorter events, 19.8 us)
Async XLA Ops:
  7.2 41.7 %copy-start = (bf16[1024,1024]{1,0:T(8,128)(2,1)S(1)}, bf16[1024,1024]{1,0:T(8,128)(2,1)}, u32[]{:S(2)}) copy-start(bf16[1024,1024]{1,0:T(8,128)(2,1)} %param.20) | copy-start | bytes 6291460
  60.2 5.6 %copy-start.12 = (bf16[1,1024]{1,0:T(2,128)(2,1)S(1)}, bf16[1,1024]{1,0:T(2,128)(2,1)}, u32[]{:S(2)}) copy-start(bf16[1,1024]{1,0:T(2,128)(2,1)} %param.21) | copy-start | bytes 6148
  60.2 5.7 %copy-start.11 = (s32[1,2,256]{2,1,0:T(2,128)S(1)}, s32[1,2,256]{2,1,0:T(2,128)}, u32[]{:S(2)}) copy-start(s32[1,2,256]{2,1,0:T(2,128)} %param.18) | copy-start | bytes 6148
  60.2 86.3 %all-to-all-start.1 = ((bf16[48,18,1024]{2,1,0:T(8,128)(2,1)}), bf16[48,18,1024]{2,1,0:T(8,128)(2,1)}, u32[]{:S(2)}, u32[]{:S(2)}) async-start(bf16[48,18,1024]{2,1,0:T(8,128)(2,1)} %broadcast_select_fusion), calls=%async_computation.1 | async-start | bytes 4718592 | tf_op jit(solution)/shard_map/all_to_all | solution.py:80
  65.8 186.9 %all-reduce.4.cloned.1.call-start = ((), (), s32[]{:S(2)}) async-start(), calls=%async_computation.2 | async-start | bytes 1048576 | tf_op jit(solution)/shard_map/psum | solution.py:46
  154.8 108.3 %copy-start.1 = (bf16[512,1024]{1,0:T(8,128)(2,1)}, bf16[512,1024]{1,0:T(8,128)(2,1)S(1)}, u32[]{:S(2)}) copy-start(bf16[512,1024]{1,0:T(8,128)(2,1)S(1)} %gather_fusion.3) | copy-start | bytes 3145732
  157.7 7.2 %copy-start.2 = (bf16[1,128,1024]{2,1,0:T(8,128)(2,1)S(1)}, bf16[1,128,1024]{2,1,0:T(8,128)(2,1)}, u32[]{:S(2)}) copy-start(bf16[1,128,1024]{2,1,0:T(8,128)(2,1)} %param.23) | copy-start | bytes 786436
  166.9 187.4 %all-reduce.6.cloned.1.call-start = ((), (), s32[]{:S(2)}) async-start(), calls=%async_computation.3 | async-start | bytes 1048576 | tf_op jit(solution)/shard_map/psum | solution.py:46
  252.7 11.5 %copy-start.13 = (bf16[1,1024,4,128]{3,2,1,0:T(4,128)(2,1)S(1)}, bf16[1,1024,4,128]{3,2,1,0:T(4,128)(2,1)}, u32[]{:S(2)}) copy-start(bf16[1,1024,4,128]{3,2,1,0:T(4,128)(2,1)} %param.22) | copy-start | bytes 3145732
  254.1 9.1 %collective-permute-start = (bf16[256,1024]{1,0:T(8,128)(2,1)S(1)}, bf16[256,1024]{1,0:T(8,128)(2,1)S(1)}, u32[]{:S(2)}, u32[]{:S(2)}) collective-permute-start(bf16[256,1024]{1,0:T(8,128)(2,1)S(1)} %fusion.9), channel_id=1, source_target_pairs={{1,0},{0,1},{3,2},{2,3},{5,4},{4,5},{7,6},{6,7},{9,8},{8,9},{11,10... | collective-permute-start | bytes 1572872 | tf_op jit(solution)/shard_map/ppermute | solution.py:17
  263.4 0.8 copy-start.3
  264.9 89.5 %copy-start.4 = (bf16[256,1024]{1,0:T(8,128)(2,1)S(1)}, bf16[256,1024]{1,0:T(8,128)(2,1)}, u32[]{:S(2)}) copy-start(bf16[256,1024]{1,0:T(8,128)(2,1)} %copy-done.3) | copy-start | bytes 1572868
  268.5 190.4 %all-reduce.8.cloned.1.call-start = ((), (), s32[]{:S(2)}) async-start(), calls=%async_computation.4 | async-start | bytes 1048576 | tf_op jit(solution)/shard_map/psum | solution.py:46
  354.4 12.7 %copy-start.14 = (bf16[1,1024,4,128]{3,2,1,0:T(4,128)(2,1)S(1)}, bf16[1,1024,4,128]{3,2,1,0:T(4,128)(2,1)}, u32[]{:S(2)}) copy-start(bf16[1,1024,4,128]{3,2,1,0:T(4,128)(2,1)} %param.22) | copy-start | bytes 3145732
  355.7 9.1 %collective-permute-start.1 = (bf16[256,1024]{1,0:T(8,128)(2,1)S(1)}, bf16[256,1024]{1,0:T(8,128)(2,1)S(1)}, u32[]{:S(2)}, u32[]{:S(2)}) collective-permute-start(bf16[256,1024]{1,0:T(8,128)(2,1)S(1)} %fusion.13), channel_id=1, source_target_pairs={{1,0},{0,1},{3,2},{2,3},{5,4},{4,5},{7,6},{6,7},{9,8},{8,9},{11,10... | collective-permute-start | bytes 1572872 | tf_op jit(solution)/shard_map/ppermute | solution.py:17
  364.8 1.5 copy-start.5
  366.3 0.8 copy-start.7
  369.4 3.6 copy-start.10
  373.0 85.9 %copy-start.6 = (bf16[256,1024]{1,0:T(8,128)(2,1)S(1)}, bf16[256,1024]{1,0:T(8,128)(2,1)}, u32[]{:S(2)}) copy-start(bf16[256,1024]{1,0:T(8,128)(2,1)} %copy-done.5) | copy-start | bytes 1572868
  383.0 4.4 copy-start.15
  383.0 4.4 copy-start.9
  387.7 73.5 %copy-start.8 = (bf16[1024,128]{1,0:T(8,128)(2,1)S(1)}, bf16[1024,128]{1,0:T(8,128)(2,1)}, u32[]{:S(2)}) copy-start(bf16[1024,128]{1,0:T(8,128)(2,1)} %param.24) | copy-start | bytes 786436
  387.8 88.1 %collective-permute-start.2 = (bf16[256,128]{1,0:T(8,128)(2,1)S(1)}, bf16[256,128]{1,0:T(8,128)(2,1)S(1)}, u32[]{:S(2)}, u32[]{:S(2)}) collective-permute-start(bf16[256,128]{1,0:T(8,128)(2,1)S(1)} %get-tuple-element.122), channel_id=1, source_target_pairs={{1,0},{0,1},{3,2},{2,3},{5,4},{4,5},{7,6},{6,7},{9,8},{8,9},{11,10... | collective-permute-start | bytes 196616 | tf_op jit(solution)/shard_map/ppermute | solution.py:17
  471.2 4.4 copy-start.16
Sparse Core Ops, SparseCore 0:
  167.1 85.6 all-reduce.3
  268.6 85.6 all-reduce.5
  373.1 85.6 all-reduce.7
where the time goes:
time: 484 us; the launch traced here: 483 us
  waiting for transfers between devices  324 us (67%)
  local copies, waits for them, and re-layouts  50.1 us (10%)
  blocking collectives  34.8 us (7%)
  other arithmetic  23.3 us (5%)
  starting transfers between devices  23 us (5%)
  matrix products  14.1 us (3%)
  between operations  14.1 us (3%)
    psum x3, waiting for transfers between devices, hstu_local(): lax.psum(partial_term.astype(jnp.bfloat16), 'mp').astype(jnp.float32)  241 us
    all_to_all x1, waiting for transfers between devices, on_device(): lax.all_to_all(found, 'dp', split_axis=0, concat_axis=0, tiled=True)  80 us
    all_to_all x1, blocking collectives, on_device(): lax.all_to_all(requests, 'dp', split_axis=0, concat_axis=0, tiled=True)  34.8 us
    gather x2, local copies, waits for them, and re-layouts, context_local(): jnp.take(states, neigh_rows.reshape(-1), axis=0).astype(jnp.float32)  19.3 us
    ppermute x3, starting transfers between devices, passed_along(): return lax.ppermute(block, axis, route)  17.3 us
  transfers between devices with their start and end apart: 7, of which 6 were waited for; matrix products, arithmetic and copies ran while one was open for 7% of the time, Pallas kernels for 0%

commit v1 on v0

v1 whole, which is shorter than its diff:
```python
import functools

import jax
import jax.numpy as jnp
from jax import lax
from jax.experimental import pallas as pl
from jax.experimental.pallas import tpu as pltpu
from jax.sharding import PartitionSpec as P

MESH = pl.DeviceIdType.MESH
F32 = jnp.float32
BF16 = jnp.bfloat16
I32 = jnp.int32

D = 1024
HD = 128
NBR = 8
ROWS = 256
MP = 8
ZN = 12
YN = 4
PEERS = ZN // 2 * YN
SLOTS = 32
OWN = ROWS // MP
EPS = 1e-06


def silu(x):
    half = 0.5 * x
    return half * (1.0 + jnp.tanh(half))


def iota(shape, axis):
    return lax.broadcasted_iota(I32, shape, axis)


def to_column(row):
    n = row.shape[1]
    diag = iota((n, n), 0) == iota((n, n), 1)
    return jnp.sum(jnp.where(diag, jnp.broadcast_to(row, (n, n)), 0.0), axis=1, keepdims=True)


def kernel(
    owner_ref, item_ref, seg_ref, nbr_ref, gain_ref, bias_ref, table_hbm, w_hbm, wo_hbm, wctx_hbm,
    out_hbm, ctx_ref,
    tcol, w4, wp, wo, wctx, gbuf, reqout, reqin, repout, repin, pick, part0, partin, xcols,
    mask, counts, nrm, part, rsin, xrow, states,
    loc, req_s, req_r, rep_s, rep_r, wex_s, wex_r, xp_s, xp_r, ag_s, ag_r, rs_s, rs_r, out_s,
):
    g = lax.axis_index("dp")
    m = lax.axis_index("mp")
    p = lax.axis_index("phase")
    q = 1 - p
    zg, yg = g // YN, g % YN
    slot_me = (zg // 2) * YN + yg
    is_even = p == 0

    def dp_peer(j, dy):
        z = lax.rem(zg + 2 * j + p, ZN)
        y = lax.rem(yg + dy, YN)
        return z * YN + y, (z // 2) * YN + y

    def mp_peer(d):
        return lax.rem(m + d, MP)

    def remote(src, dst, s, r, dev):
        return pltpu.make_async_remote_copy(
            src_ref=src, dst_ref=dst, send_sem=s, recv_sem=r, device_id=dev, device_id_type=MESH
        )

    def drain(ref, sem):
        pltpu.make_async_copy(ref, ref, sem).wait()

    barrier = pltpu.get_barrier_semaphore()

    def greet(dev):
        pl.semaphore_signal(barrier, inc=1, device_id=dev, device_id_type=MESH)

    far_first = (3, 2, 4, 1, 5, 0)
    for j in far_first:
        for dy in (2, 1, 3, 0):
            o, _ = dp_peer(j, dy)
            if (j, dy) == (0, 0):
                @pl.when(p == 1)
                def _():
                    greet((o, m, p))
            else:
                greet((o, m, p))
    for d in range(1, MP):
        greet((g, mp_peer(d), p))
    greet((g, m, q))

    col0 = pl.multiple_of(m * HD, HD)
    loads = [
        pltpu.make_async_copy(table_hbm.at[:, pl.ds(col0, HD)], tcol, loc.at[0]),
        pltpu.make_async_copy(w_hbm, w4.at[p], loc.at[1]),
        pltpu.make_async_copy(wo_hbm, wo.at[p], loc.at[2]),
        pltpu.make_async_copy(wctx_hbm, wctx, loc.at[3]),
    ]
    for load in loads:
        load.start()
    gbuf[p] = jnp.broadcast_to(gain_ref[...].astype(F32), (8, D))

    n_rows = owner_ref.shape[1]
    owners = owner_ref[...]
    items = item_ref[...]
    slot_col = iota((PEERS, n_rows), 0)
    owner_of_slot = (2 * (slot_col // YN) + lax.rem(zg + p, 2)) * YN + slot_col % YN
    hit = (jnp.broadcast_to(owners, (PEERS, n_rows)) == owner_of_slot).astype(F32)
    before = (iota((n_rows, n_rows), 0) < iota((n_rows, n_rows), 1)).astype(F32).astype(BF16)
    count = jnp.dot(hit.astype(BF16), before, preferred_element_type=F32)
    rank = jnp.sum(hit * count, axis=0, keepdims=True)
    mine = jnp.sum(hit, axis=0, keepdims=True)
    slot_row = jnp.sum(hit * slot_col.astype(F32), axis=0, keepdims=True)
    key = jnp.where(mine > 0.5, slot_row * SLOTS + rank, -1.0)
    ranked = jnp.where(mine > 0.5, rank, -1.0)
    at_rank = (iota((HD, n_rows), 0).astype(F32) == jnp.broadcast_to(ranked, (HD, n_rows)))
    at_rank = at_rank.astype(F32).astype(BF16)
    hi = (items >> 5).astype(F32)
    lo = (items & 31).astype(F32)
    both = jnp.concatenate([hit * hi, hit * lo], axis=0).astype(BF16)
    found = lax.dot_general(both, at_rank, (((1,), (1,)), ((), ())), preferred_element_type=F32)
    wanted = (found[:PEERS] * 32.0 + found[PEERS:]).astype(I32)
    for s in range(PEERS):
        reqout[s] = wanted[s : s + 1]

    pl.semaphore_wait(barrier, 31 + p)

    def to_peers(src_of, dst, s_sem, r_sem, js):
        for j in js:
            for dy in (2, 1, 3, 0):
                o, s = dp_peer(j, dy)
                if (j, dy) == (0, 0):
                    @pl.when(is_even)
                    def _():
                        pltpu.make_async_copy(src_of.at[s], dst.at[slot_me], r_sem).start()

                    @pl.when(p == 1)
                    def _():
                        remote(src_of.at[s], dst.at[slot_me], s_sem, r_sem, (o, m, p)).start()
                else:
                    remote(src_of.at[s], dst.at[slot_me], s_sem, r_sem, (o, m, p)).start()

    to_peers(reqout, reqin, req_s, req_r, far_first)

    loads[1].wait()
    loads[2].wait()
    sibling = (g, m, q)
    exchange = [
        remote(w4.at[p], w4.at[p], wex_s.at[0], wex_r.at[0], sibling),
        remote(wo.at[p], wo.at[p], wex_s.at[1], wex_r.at[1], sibling),
        remote(gbuf.at[p], gbuf.at[p], wex_s.at[2], wex_r.at[2], sibling),
    ]
    for copy in exchange:
        copy.start()

    per_chunk = 64
    src_col = iota((4 * per_chunk, 4 * per_chunk), 1)
    dst_row = iota((4 * per_chunk, 4 * per_chunk), 0)
    spread = (src_col == 4 * (dst_row % per_chunk) + dst_row // per_chunk).astype(F32).astype(BF16)

    def arrange(sec):
        def body(i, carry):
            base = pl.multiple_of(i * 4 * per_chunk, 4 * per_chunk)
            moved = jnp.dot(spread, w4[sec, pl.ds(base, 4 * per_chunk), :], preferred_element_type=F32)
            moved = moved.astype(BF16)
            to = pl.multiple_of(i * per_chunk, per_chunk)
            for c in range(4):
                wp[sec, pl.ds(to, per_chunk), c * HD : (c + 1) * HD] = moved[
                    c * per_chunk : (c + 1) * per_chunk
                ]
            return carry

        lax.fori_loop(0, D // per_chunk, body, 0)

    arrange(p)
    key_col = to_column(key)
    for h in range(2):
        lanes = iota((ROWS, PEERS * SLOTS), 1).astype(F32)
        pick[h] = (key_col[h * ROWS : (h + 1) * ROWS] == lanes).astype(F32).astype(BF16)

    loads[0].wait()
    drain(reqin, req_r)
    for pair in ((3, 2), (4, 1), (5, 0)):
        columns = []
        for j in pair:
            z = lax.rem(zg + 2 * j + p, ZN)
            base = (z // 2) * YN
            asked = jnp.broadcast_to(reqin[pl.ds(base, YN)], (YN, SLOTS, HD))
            on = iota((YN, SLOTS, HD), 1) == iota((YN, SLOTS, HD), 2)
            columns.append(
                jnp.sum(jnp.where(on, asked.astype(F32), 0.0), axis=2, keepdims=True).reshape(
                    YN * SLOTS, 1
                )
            )
        column = jnp.concatenate(columns, axis=0)
        size = 2 * YN * SLOTS
        hot = (column == iota((size, D), 1).astype(F32)).astype(F32).astype(BF16)
        rows = jnp.dot(hot, tcol[...], preferred_element_type=F32).astype(BF16)
        rows = rows.reshape(2, YN, SLOTS, HD)
        for i, j in enumerate(pair):
            z = lax.rem(zg + 2 * j + p, ZN)
            repout[pl.ds((z // 2) * YN, YN)] = rows[i]
        to_peers(repout, repin, rep_s, rep_r, pair)

    exchange[0].wait_recv()
    exchange[1].wait_recv()
    exchange[2].wait_recv()
    arrange(q)
    seg = seg_ref[pl.ds(p, 1), :].astype(F32)
    seg_col = to_column(seg)
    below = iota((ROWS, ROWS), 1) <= iota((ROWS, ROWS), 0)
    same = seg_col == jnp.broadcast_to(seg, (ROWS, ROWS))
    mask[...] = jnp.where(below & same, 1.0 / ROWS, 0.0)
    hits = jnp.zeros((ROWS, ROWS), F32)
    near = nbr_ref[p]
    for n in range(NBR):
        row = jnp.broadcast_to(near[n : n + 1], (ROWS, ROWS))
        hits = hits + jnp.where(row == iota((ROWS, ROWS), 0), 1.0 / NBR, 0.0)
    counts[...] = hits.T.astype(BF16)

    drain(repin, rep_r)
    for h in range(2):
        part0[h] = jnp.dot(
            pick[h], repin[...].reshape(PEERS * SLOTS, HD), preferred_element_type=F32
        ).astype(BF16)
    swap = remote(part0.at[q], partin, xp_s, xp_r, sibling)
    swap.start()
    swap.wait_recv()
    xcols[m] = part0[p] + partin[...]

    def to_group(src_of, dst, s_sem, r_of):
        for d in (4, 2, 6, 5, 7, 1, 3):
            to = mp_peer(d)
            remote(src_of(to), dst, s_sem, r_of, (g, to, p)).start()

    to_group(lambda to: xcols.at[m], xcols.at[m], ag_s.at[0], ag_r.at[0])
    drain(xcols.at[pl.ds(0, MP - 1)], ag_r.at[0])

    total = jnp.zeros((ROWS, 1), F32)
    for k in range(MP):
        block = xcols[k].astype(F32)
        total = total + jnp.sum(block * block, axis=1, keepdims=True)
    inv = lax.rsqrt(total * (1.0 / D) + EPS)
    for k in range(MP):
        scaled = xcols[k].astype(F32) * inv * gbuf[0, 0:1, k * HD : (k + 1) * HD]
        nrm[0, :, :, k * HD : (k + 1) * HD] = scaled.astype(BF16).reshape(MP, OWN, HD)
    own_row = pl.multiple_of(m * OWN, OWN)
    for k in range(MP):
        xrow[:, k * HD : (k + 1) * HD] = xcols[k, pl.ds(own_row, OWN), :].astype(F32)

    for sec in range(2):
        proj = jnp.dot(
            nrm[sec].reshape(ROWS, D), wp[sec], preferred_element_type=F32
        )
        proj = silu(proj).astype(BF16)
        gate, value = proj[:, :HD], proj[:, HD : 2 * HD]
        query, keys = proj[:, 2 * HD : 3 * HD], proj[:, 3 * HD :]
        scores = lax.dot_general(
            query, keys, (((1,), (1,)), ((), ())), preferred_element_type=F32
        ) * HD ** (-0.5)
        attn = (silu(scores) * mask[...]).astype(BF16)
        mixed = jnp.dot(attn, value, preferred_element_type=F32)
        mixed = mixed * lax.rsqrt(jnp.mean(mixed * mixed, axis=1, keepdims=True) + EPS)
        gated = (mixed * gate.astype(F32)).astype(BF16)
        back = jnp.dot(gated, wo[sec], preferred_element_type=F32).astype(BF16)
        part[sec] = back.reshape(MP, OWN, D)
        to_group(
            lambda to: part.at[sec, to], rsin.at[sec, m], rs_s.at[sec], rs_r.at[sec, m]
        )
        acc = part[sec, m].astype(F32)
        for d in (1, 3, 5, 7, 2, 6, 4):
            src = mp_peer(d)
            drain(rsin.at[sec, src], rs_r.at[sec, src])
            acc = acc + rsin[sec, src].astype(F32)
        new = (xrow[...] + acc).astype(BF16)
        if sec == 0:
            newf = new.astype(F32)
            xrow[...] = newf
            inv = lax.rsqrt(jnp.mean(newf * newf, axis=1, keepdims=True) + EPS)
            nrm[1, m] = (newf * inv * gbuf[1, 0:1, :]).astype(BF16)
            to_group(lambda to: nrm.at[1, m], nrm.at[1, m], ag_s.at[1], ag_r.at[1])
            drain(nrm.at[1, pl.ds(0, MP - 1)], ag_r.at[1])
        else:
            states[m] = new
            to_group(lambda to: states.at[m], states.at[m], ag_s.at[2], ag_r.at[2])
            drain(states.at[pl.ds(0, MP - 1)], ag_r.at[2])

    write = pltpu.make_async_copy(states, out_hbm, out_s)
    write.start()
    loads[3].wait()
    scored = jnp.dot(
        states[...].reshape(ROWS, D), wctx[...], preferred_element_type=F32
    ).astype(BF16)
    summed = jnp.dot(counts[...], scored, preferred_element_type=F32)
    ctx_ref[...] = silu(summed + bias_ref[...].astype(F32)).astype(BF16)

    for copy in exchange:
        copy.wait_send()
    swap.wait_send()

    @pl.when(is_even)
    def _():
        drain(reqout.at[pl.ds(0, PEERS - 1)], req_s)
        drain(repout.at[pl.ds(0, PEERS - 1)], rep_s)

    @pl.when(p == 1)
    def _():
        drain(reqout, req_s)
        drain(repout, rep_s)

    drain(xcols.at[pl.ds(0, MP - 1)], ag_s.at[0])
    drain(nrm.at[1, pl.ds(0, MP - 1)], ag_s.at[1])
    drain(states.at[pl.ds(0, MP - 1)], ag_s.at[2])
    for sec in range(2):
        drain(part.at[sec, pl.ds(0, MP - 1)], rs_s.at[sec])
    write.wait()


def on_device(
    item_owner, item_row, segments, neighbors, table, gains, w_in, w_out, w_ctx, ctx_bias
):
    n_rows = item_row.shape[0]
    vmem = pl.BlockSpec(memory_space=pltpu.VMEM)
    hbm = pl.BlockSpec(memory_space=pl.ANY)
    dma = pltpu.SemaphoreType.DMA
    states, ctx = pl.pallas_call(
        kernel,
        out_shape=(
            jax.ShapeDtypeStruct((MP, OWN, D), BF16),
            jax.ShapeDtypeStruct((ROWS, HD), BF16),
        ),
        in_specs=[vmem] * 6 + [hbm] * 4,
        out_specs=(hbm, vmem),
        scratch_shapes=[
            pltpu.VMEM((D, HD), BF16),
            pltpu.VMEM((2, 4 * D, HD), BF16),
            pltpu.VMEM((2, D, 4 * HD), BF16),
            pltpu.VMEM((2, HD, D), BF16),
            pltpu.VMEM((D, HD), BF16),
            pltpu.VMEM((2, 8, D), F32),
            pltpu.VMEM((PEERS, 1, HD), I32),
            pltpu.VMEM((PEERS, 1, HD), I32),
            pltpu.VMEM((PEERS, SLOTS, HD), BF16),
            pltpu.VMEM((PEERS, SLOTS, HD), BF16),
            pltpu.VMEM((2, ROWS, PEERS * SLOTS), BF16),
            pltpu.VMEM((2, ROWS, HD), BF16),
            pltpu.VMEM((ROWS, HD), BF16),
            pltpu.VMEM((MP, ROWS, HD), BF16),
            pltpu.VMEM((ROWS, ROWS), F32),
            pltpu.VMEM((ROWS, ROWS), BF16),
            pltpu.VMEM((2, MP, OWN, D), BF16),
            pltpu.VMEM((2, MP, OWN, D), BF16),
            pltpu.VMEM((2, MP, OWN, D), BF16),
            pltpu.VMEM((OWN, D), F32),
            pltpu.VMEM((MP, OWN, D), BF16),
            dma((4,)),
            dma(()),
            dma(()),
            dma(()),
            dma(()),
            dma((3,)),
            dma((3,)),
            dma(()),
            dma(()),
            dma((3,)),
            dma((3,)),
            dma((2,)),
            dma((2, MP)),
            dma(()),
        ],
        compiler_params=pltpu.CompilerParams(
            collective_id=0, has_side_effects=True, vmem_limit_bytes=60 * 1024 * 1024
        ),
        name="cascade",
    )(
        item_owner.reshape(1, n_rows),
        item_row.reshape(1, n_rows),
        segments[0],
        jnp.swapaxes(neighbors[0], 1, 2),
        gains,
        ctx_bias.reshape(1, -1),
        table,
        w_in.reshape(4 * D, HD),
        w_out[0],
        w_ctx,
    )
    return states.reshape(1, 1, ROWS, D), ctx.reshape(1, 1, ROWS, HD)


def solution(mesh):
    in_specs = (
        P("dp", None),
        P("dp"),
        P("dp", None, None),
        P("dp", None, None, None),
        P("dp", None),
        P("phase", None),
        P("phase", None, None, "mp"),
        P("phase", "mp", None),
        P(None, "mp"),
        P("mp"),
    )
    out_specs = (P("dp", "phase", None, None), P("dp", "phase", None, "mp"))
    return jax.shard_map(
        on_device, mesh=mesh, in_specs=in_specs, out_specs=out_specs, check_vma=False
    )
```

time: 484 us -> 88.5 us (0.18)
  waiting for transfers between devices: 324 us -> 0 us
  Pallas kernels: 0 us -> 84.3 us
  local copies, waits for them, and re-layouts: 50.1 us -> 3.34 us
  blocking collectives: 34.8 us -> 0 us
  other arithmetic: 23.3 us -> 0 us
  starting transfers between devices: 23 us -> 0 us
  matrix products: 14.1 us -> 0 us
  between operations: 14.1 us -> 0.64 us
    psum x3 -> x0, waiting for transfers between devices: 241 us -> none  [hstu_local(): lax.psum(partial_term.astype(jnp.bfloat16), 'mp').astype(jnp.float32)]
    pallas_call x0 -> x1, Pallas kernels: none -> 84.3 us  [on_device(): pl.pallas_call(kernel, out_shape=(jax.ShapeDtypeStruct((MP, OWN, D), BF16...]
    all_to_all x1 -> x0, waiting for transfers between devices: 80 us -> none  [on_device(): lax.all_to_all(found, 'dp', split_axis=0, concat_axis=0, tiled=True)]
    all_to_all x1 -> x0, blocking collectives: 34.8 us -> none  [on_device(): lax.all_to_all(requests, 'dp', split_axis=0, concat_axis=0, tiled=True)]
    gather x5 -> x0, local copies, waits for them, and re-layouts: 31.7 us -> none  [the longest x2 19.3 us: context_local(): jnp.take(states, neigh_rows.reshape(-1), axis=0).astype(jnp.float32)]
    ppermute x3 -> x0, starting transfers between devices: 17.3 us -> none  [passed_along(): return lax.ppermute(block, axis, route)]
    dot_general x11 -> x0, matrix products: 14.1 us -> none  [the longest x3 4.72 us: hstu_local(): jnp.einsum('hqk,khd->qhd', weights, values_h, preferred_element_type=jnp....]
    reduce_sum x6 -> x0, other arithmetic: 11.5 us -> none  [the longest x2 8.71 us: context_local(): jnp.mean(picked.reshape(neigh_rows.shape[0], NBR, states.shape[1]), axis=1)]
  transfers between devices with their start and end apart: 7 -> 0, of which waited for: 6 -> 0; matrix products, arithmetic and copies ran while one was open for 7% -> 0% of each run, Pallas kernels for 0% -> 0%
where the time goes in v1:
time: 88.5 us; the launch traced here: 88.3 us
  Pallas kernels  84.3 us (95%)
  local copies, waits for them, and re-layouts  3.34 us (4%)
    pallas_call x1, Pallas kernels, on_device(): pl.pallas_call(kernel, out_shape=(jax.ShapeDtypeStruct((MP, OWN, D), BF16...  84.3 us
    unnamed x2, local copies, waits for them, and re-layouts  3.34 us

profile of v1, /device:TPU:1, one launch (start us, length us, event | category | flops | bytes accessed | tf_op | source)
XLA Modules:
  0.0 88.3 jit_solution(1566768595821131620)
XLA Ops:
  0.6 84.3 %cascade.1 = (bf16[8,32,1024]{2,1,0:T(8,128)(2,1)}, bf16[256,128]{1,0:T(8,128)(2,1)}) custom-call(s32[1,512]{1,0:T(1,128)} %bitcast.16, s32[1,512]{1,0:T(1,128)} %bitcast.17, s32[2,256]{1,0:T(2,128)} %bitcast.18, s32[2,8,256]{2,1,0:T(8,128)} %bitcast.15, bf16[1,1024]{1,0:T(2,128)(2,1)} %gain_ref.1, bf16[1,128]{1,0:T(2,128)(2,1)} %bitcast.19, ...), custom_call_target="tpu_custom_call" | custom-call | tf_op jit(solution)/shard_map/cascade/pallas_call | solution.py:327
  84.9 1.9 %copy.14 = bf16[1,1,256,1024]{3,2,1,0:T(8,128)(2,1)} copy(bf16[1,1,256,1024]{3,2,1,0:T(8,128)(2,1)} %bitcast.12) | data formatting | bytes 1048576
  86.8 1.5 %copy.15 = bf16[1,1,256,128]{3,2,1,0:T(8,128)(2,1)} copy(bf16[1,1,256,128]{3,2,1,0:T(8,128)(2,1)} %bitcast.14) | data formatting | bytes 131072

commit v2 on v1

--- a/solution.py
+++ b/solution.py
@@ -43,9 +43,10 @@
 def kernel(
     owner_ref, item_ref, seg_ref, nbr_ref, gain_ref, bias_ref, table_hbm, w_hbm, wo_hbm, wctx_hbm,
     out_hbm, ctx_ref,
-    tcol, w4, wp, wo, wctx, gbuf, reqout, reqin, repout, repin, pick, part0, partin, xcols,
-    mask, counts, nrm, part, rsin, xrow, states,
-    loc, req_s, req_r, rep_s, rep_r, wex_s, wex_r, xp_s, xp_r, ag_s, ag_r, rs_s, rs_r, out_s,
+    tcol, w4, wp, wo, wctx, gbuf, reqout, reqin, repout, repin, pick, part0, partin, xown, xcols,
+    mask, counts, nrm, part, pairin, pairsum, rsin, xrow, last, states,
+    loc, req_s, req_r, rep_s, rep_r, wex_s, wex_r, gex_s, gex_r, xp_s, xp_r, ag_s, ag0_r, ag1_r,
+    pair_s, pair_r, rs_s, rs_r, fin_s, fin_r, out_s,
 ):
     g = lax.axis_index("dp")
     m = lax.axis_index("mp")
@@ -54,14 +55,26 @@
     zg, yg = g // YN, g % YN
     slot_me = (zg // 2) * YN + yg
     is_even = p == 0
+    y, x = m // 4, m % 4
+    batch = x // 2
+    i = x % 2
+    chip = 2 * y + i
+    m_x = m + 1 - 2 * i
+    m_y = lax.rem(m + 4, MP)
+    m_d = lax.rem(m_x + 4, MP)
+    near_m = (m_x, m_y, m_d)
+    near_chip = (2 * y + 1 - i, 2 * (1 - y) + i, 2 * (1 - y) + 1 - i)
+    twin = 4 * y + 3 - x
+    block = 4 * p + chip
+    at_home = p == batch
+    away = p != batch
+    sibling = (g, m, q)
 
     def dp_peer(j, dy):
         z = lax.rem(zg + 2 * j + p, ZN)
-        y = lax.rem(yg + dy, YN)
-        return z * YN + y, (z // 2) * YN + y
-
-    def mp_peer(d):
-        return lax.rem(m + d, MP)
+        yy = lax.rem(yg + dy, YN)
+        o = z * YN + yy
+        return (o, m_y if dy == 2 else m, p), (z // 2) * YN + yy
 
     def remote(src, dst, s, r, dev):
         return pltpu.make_async_remote_copy(
@@ -77,28 +90,38 @@
         pl.semaphore_signal(barrier, inc=1, device_id=dev, device_id_type=MESH)
 
     far_first = (3, 2, 4, 1, 5, 0)
+    dy_order = (2, 1, 3, 0)
     for j in far_first:
-        for dy in (2, 1, 3, 0):
-            o, _ = dp_peer(j, dy)
+        for dy in dy_order:
+            dev, _ = dp_peer(j, dy)
             if (j, dy) == (0, 0):
                 @pl.when(p == 1)
                 def _():
-                    greet((o, m, p))
+                    greet(dev)
             else:
-                greet((o, m, p))
+                greet(dev)
     for d in range(1, MP):
-        greet((g, mp_peer(d), p))
-    greet((g, m, q))
-
-    col0 = pl.multiple_of(m * HD, HD)
-    loads = [
-        pltpu.make_async_copy(table_hbm.at[:, pl.ds(col0, HD)], tcol, loc.at[0]),
-        pltpu.make_async_copy(w_hbm, w4.at[p], loc.at[1]),
-        pltpu.make_async_copy(wo_hbm, wo.at[p], loc.at[2]),
-        pltpu.make_async_copy(wctx_hbm, wctx, loc.at[3]),
-    ]
+        for core in range(2):
+            greet((g, lax.rem(m + d, MP), core))
+    greet(sibling)
+
+    loads = []
+    for n, column in enumerate((m, m_y)):
+        col0 = pl.multiple_of(column * HD, HD)
+        loads.append(
+            pltpu.make_async_copy(
+                table_hbm.at[:, pl.ds(col0, HD)], tcol.at[:, n * HD : (n + 1) * HD], loc.at[n]
+            )
+        )
+    loads.append(pltpu.make_async_copy(wctx_hbm, wctx, loc.at[2]))
     for load in loads:
         load.start()
+
+    @pl.when(is_even)
+    def _():
+        pltpu.make_async_copy(w_hbm, w4.at[0], wex_r.at[0, 0]).start()
+        pltpu.make_async_copy(wo_hbm, wo.at[0], wex_r.at[1, 0]).start()
+
     gbuf[p] = jnp.broadcast_to(gain_ref[...].astype(F32), (8, D))
 
     n_rows = owner_ref.shape[1]
@@ -124,12 +147,12 @@
     for s in range(PEERS):
         reqout[s] = wanted[s : s + 1]
 
-    pl.semaphore_wait(barrier, 31 + p)
+    pl.semaphore_wait(barrier, 38 + p)
 
     def to_peers(src_of, dst, s_sem, r_sem, js):
         for j in js:
-            for dy in (2, 1, 3, 0):
-                o, s = dp_peer(j, dy)
+            for dy in dy_order:
+                dev, s = dp_peer(j, dy)
                 if (j, dy) == (0, 0):
                     @pl.when(is_even)
                     def _():
@@ -137,22 +160,26 @@
 
                     @pl.when(p == 1)
                     def _():
-                        remote(src_of.at[s], dst.at[slot_me], s_sem, r_sem, (o, m, p)).start()
+                        remote(src_of.at[s], dst.at[slot_me], s_sem, r_sem, dev).start()
                 else:
-                    remote(src_of.at[s], dst.at[slot_me], s_sem, r_sem, (o, m, p)).start()
+                    remote(src_of.at[s], dst.at[slot_me], s_sem, r_sem, dev).start()
 
     to_peers(reqout, reqin, req_s, req_r, far_first)
 
-    loads[1].wait()
-    loads[2].wait()
-    sibling = (g, m, q)
-    exchange = [
-        remote(w4.at[p], w4.at[p], wex_s.at[0], wex_r.at[0], sibling),
-        remote(wo.at[p], wo.at[p], wex_s.at[1], wex_r.at[1], sibling),
-        remote(gbuf.at[p], gbuf.at[p], wex_s.at[2], wex_r.at[2], sibling),
-    ]
-    for copy in exchange:
-        copy.start()
+    def send_weights(sec, dev):
+        remote(w_hbm, w4.at[sec], wex_s.at[0], wex_r.at[0, sec], dev).start()
+        remote(wo_hbm, wo.at[sec], wex_s.at[1], wex_r.at[1, sec], dev).start()
+
+    gains = remote(gbuf.at[p], gbuf.at[p], gex_s, gex_r, sibling)
+    gains.start()
+
+    @pl.when(is_even)
+    def _():
+        send_weights(0, (g, twin, 1))
+
+    @pl.when(p == 1)
+    def _():
+        send_weights(1, (g, m, 0))
 
     per_chunk = 64
     src_col = iota((4 * per_chunk, 4 * per_chunk), 1)
@@ -160,11 +187,14 @@
     spread = (src_col == 4 * (dst_row % per_chunk) + dst_row // per_chunk).astype(F32).astype(BF16)
 
     def arrange(sec):
-        def body(i, carry):
-            base = pl.multiple_of(i * 4 * per_chunk, 4 * per_chunk)
+        drain(w4.at[sec], wex_r.at[0, sec])
+        drain(wo.at[sec], wex_r.at[1, sec])
+
+        def body(n, carry):
+            base = pl.multiple_of(n * 4 * per_chunk, 4 * per_chunk)
             moved = jnp.dot(spread, w4[sec, pl.ds(base, 4 * per_chunk), :], preferred_element_type=F32)
             moved = moved.astype(BF16)
-            to = pl.multiple_of(i * per_chunk, per_chunk)
+            to = pl.multiple_of(n * per_chunk, per_chunk)
             for c in range(4):
                 wp[sec, pl.ds(to, per_chunk), c * HD : (c + 1) * HD] = moved[
                     c * per_chunk : (c + 1) * per_chunk
@@ -173,19 +203,19 @@
 
         lax.fori_loop(0, D // per_chunk, body, 0)
 
-    arrange(p)
     key_col = to_column(key)
     for h in range(2):
         lanes = iota((ROWS, PEERS * SLOTS), 1).astype(F32)
         pick[h] = (key_col[h * ROWS : (h + 1) * ROWS] == lanes).astype(F32).astype(BF16)
 
     loads[0].wait()
+    loads[1].wait()
     drain(reqin, req_r)
+    crossed = lax.rem(yg + 2, YN)
     for pair in ((3, 2), (4, 1), (5, 0)):
         columns = []
         for j in pair:
-            z = lax.rem(zg + 2 * j + p, ZN)
-            base = (z // 2) * YN
+            base = (lax.rem(zg + 2 * j + p, ZN) // 2) * YN
             asked = jnp.broadcast_to(reqin[pl.ds(base, YN)], (YN, SLOTS, HD))
             on = iota((YN, SLOTS, HD), 1) == iota((YN, SLOTS, HD), 2)
             columns.append(
@@ -196,18 +226,20 @@
         column = jnp.concatenate(columns, axis=0)
         size = 2 * YN * SLOTS
         hot = (column == iota((size, D), 1).astype(F32)).astype(F32).astype(BF16)
-        rows = jnp.dot(hot, tcol[...], preferred_element_type=F32).astype(BF16)
+        rows = jnp.dot(hot, tcol[...], preferred_element_type=F32)
+        group = (iota((size, HD), 0) // SLOTS) % YN
+        rows = jnp.where(group == crossed, rows[:, HD:], rows[:, :HD]).astype(BF16)
         rows = rows.reshape(2, YN, SLOTS, HD)
-        for i, j in enumerate(pair):
-            z = lax.rem(zg + 2 * j + p, ZN)
-            repout[pl.ds((z // 2) * YN, YN)] = rows[i]
+        for n, j in enumerate(pair):
+            base = (lax.rem(zg + 2 * j + p, ZN) // 2) * YN
+            repout[pl.ds(base, YN)] = rows[n]
         to_peers(repout, repin, rep_s, rep_r, pair)
 
-    exchange[0].wait_recv()
-    exchange[1].wait_recv()
-    exchange[2].wait_recv()
-    arrange(q)
-    seg = seg_ref[pl.ds(p, 1), :].astype(F32)
+    @pl.when(p == 1)
+    def _():
+        send_weights(1, (g, twin, 1))
+
+    seg = seg_ref[pl.ds(batch, 1), :].astype(F32)
     seg_col = to_column(seg)
     below = iota((ROWS, ROWS), 1) <= iota((ROWS, ROWS), 0)
     same = seg_col == jnp.broadcast_to(seg, (ROWS, ROWS))
@@ -218,6 +250,8 @@
         row = jnp.broadcast_to(near[n : n + 1], (ROWS, ROWS))
         hits = hits + jnp.where(row == iota((ROWS, ROWS), 0), 1.0 / NBR, 0.0)
     counts[...] = hits.T.astype(BF16)
+    arrange(0)
+    gains.wait_recv()
 
     drain(repin, rep_r)
     for h in range(2):
@@ -227,27 +261,61 @@
     swap = remote(part0.at[q], partin, xp_s, xp_r, sibling)
     swap.start()
     swap.wait_recv()
-    xcols[m] = part0[p] + partin[...]
-
-    def to_group(src_of, dst, s_sem, r_of):
-        for d in (4, 2, 6, 5, 7, 1, 3):
-            to = mp_peer(d)
-            remote(src_of(to), dst, s_sem, r_of, (g, to, p)).start()
-
-    to_group(lambda to: xcols.at[m], xcols.at[m], ag_s.at[0], ag_r.at[0])
-    drain(xcols.at[pl.ds(0, MP - 1)], ag_r.at[0])
+    own = part0[p] + partin[...]
+    xown[...] = own
+
+    @pl.when(at_home)
+    def _():
+        for to in (m_d, m_y, m_x):
+            remote(xown, xcols.at[m], ag_s.at[0], ag0_r.at[m], (g, to, y)).start()
+        remote(xown, xcols.at[m], ag_s.at[0], ag0_r.at[m], sibling).start()
+        xcols[m] = own
+
+    @pl.when(away)
+    def _():
+        for row in (1 - y, y):
+            for n in range(2):
+                to = 4 * row + 2 * p + n
+                remote(xown, xcols.at[m], ag_s.at[0], ag0_r.at[m], (g, to, y)).start()
+
+    def pass_on(src):
+        drain(xcols.at[src], ag0_r.at[src])
+        remote(xcols.at[src], xcols.at[src], ag_s.at[0], ag0_r.at[src], sibling).start()
+
+    for d in (1, 3, 2):
+        pass_on(4 * p + lax.rem(x + d, 4))
+
+    @pl.when(y != p)
+    def _():
+        pass_on(4 * p + x)
+
+    @pl.when((y != p) & away)
+    def _():
+        drain(xcols.at[m], ag0_r.at[m])
+
+    @pl.when(y == p)
+    def _():
+        drain(xcols.at[m_y], ag0_r.at[m_y])
+
+    @pl.when((y == p) & away)
+    def _():
+        drain(xcols.at[m], ag0_r.at[m])
+
+    for d in (1, 3, 2):
+        src = 4 * q + lax.rem(x + d, 4)
+        drain(xcols.at[src], ag0_r.at[src])
 
     total = jnp.zeros((ROWS, 1), F32)
-    for k in range(MP):
-        block = xcols[k].astype(F32)
-        total = total + jnp.sum(block * block, axis=1, keepdims=True)
+    for c in range(MP):
+        piece = xcols[c].astype(F32)
+        total = total + jnp.sum(piece * piece, axis=1, keepdims=True)
     inv = lax.rsqrt(total * (1.0 / D) + EPS)
-    for k in range(MP):
-        scaled = xcols[k].astype(F32) * inv * gbuf[0, 0:1, k * HD : (k + 1) * HD]
-        nrm[0, :, :, k * HD : (k + 1) * HD] = scaled.astype(BF16).reshape(MP, OWN, HD)
-    own_row = pl.multiple_of(m * OWN, OWN)
-    for k in range(MP):
-        xrow[:, k * HD : (k + 1) * HD] = xcols[k, pl.ds(own_row, OWN), :].astype(F32)
+    for c in range(MP):
+        scaled = xcols[c].astype(F32) * inv * gbuf[0, 0:1, c * HD : (c + 1) * HD]
+        nrm[0, :, :, c * HD : (c + 1) * HD] = scaled.astype(BF16).reshape(MP, OWN, HD)
+    own_row = pl.multiple_of(block * OWN, OWN)
+    for c in range(MP):
+        xrow[:, c * HD : (c + 1) * HD] = xcols[c, pl.ds(own_row, OWN), :].astype(F32)
 
     for sec in range(2):
         proj = jnp.dot(
@@ -265,39 +333,86 @@
         gated = (mixed * gate.astype(F32)).astype(BF16)
         back = jnp.dot(gated, wo[sec], preferred_element_type=F32).astype(BF16)
         part[sec] = back.reshape(MP, OWN, D)
-        to_group(
-            lambda to: part.at[sec, to], rsin.at[sec, m], rs_s.at[sec], rs_r.at[sec, m]
-        )
-        acc = part[sec, m].astype(F32)
-        for d in (1, 3, 5, 7, 2, 6, 4):
-            src = mp_peer(d)
-            drain(rsin.at[sec, src], rs_r.at[sec, src])
-            acc = acc + rsin[sec, src].astype(F32)
+        order = (near_chip[2], near_chip[1], near_chip[0], chip)
+        for c in order:
+            remote(
+                part.at[sec, 4 * q + c], pairin.at[sec, c], pair_s.at[sec], pair_r.at[sec, c], sibling
+            ).start()
+        for n in (2, 1, 0):
+            c = near_chip[n]
+            drain(pairin.at[sec, c], pair_r.at[sec, c])
+            pairsum[sec, n] = part[sec, 4 * p + c] + pairin[sec, c]
+            remote(
+                pairsum.at[sec, n], rsin.at[sec, n], rs_s.at[sec], rs_r.at[sec, n],
+                (g, near_m[n], p),
+            ).start()
+        drain(pairin.at[sec, chip], pair_r.at[sec, chip])
+        acc = part[sec, block].astype(F32) + pairin[sec, chip].astype(F32)
+        if sec == 0:
+            arrange(1)
+        for n in (0, 1, 2):
+            drain(rsin.at[sec, n], rs_r.at[sec, n])
+            acc = acc + rsin[sec, n].astype(F32)
         new = (xrow[...] + acc).astype(BF16)
         if sec == 0:
             newf = new.astype(F32)
             xrow[...] = newf
             inv = lax.rsqrt(jnp.mean(newf * newf, axis=1, keepdims=True) + EPS)
-            nrm[1, m] = (newf * inv * gbuf[1, 0:1, :]).astype(BF16)
-            to_group(lambda to: nrm.at[1, m], nrm.at[1, m], ag_s.at[1], ag_r.at[1])
-            drain(nrm.at[1, pl.ds(0, MP - 1)], ag_r.at[1])
+            nrm[1, block] = (newf * inv * gbuf[1, 0:1, :]).astype(BF16)
+            mine_now = nrm.at[1, block]
+            for n in (2, 1, 0):
+                remote(mine_now, mine_now, ag_s.at[1], ag1_r.at[block], (g, near_m[n], p)).start()
+            remote(mine_now, mine_now, ag_s.at[1], ag1_r.at[block], sibling).start()
+            for n in (0, 1, 2):
+                e = 4 * p + near_chip[n]
+                got = nrm.at[1, e]
+                drain(got, ag1_r.at[e])
+                remote(got, got, ag_s.at[1], ag1_r.at[e], sibling).start()
+            for c in (chip,) + near_chip:
+                drain(nrm.at[1, 4 * q + c], ag1_r.at[4 * q + c])
         else:
-            states[m] = new
-            to_group(lambda to: states.at[m], states.at[m], ag_s.at[2], ag_r.at[2])
-            drain(states.at[pl.ds(0, MP - 1)], ag_r.at[2])
+            last[...] = new
+            for d in (4, 2, 6, 5, 7, 1, 3):
+                to = lax.rem(m + d, MP)
+                remote(last, states.at[block], fin_s, fin_r, (g, to, batch)).start()
+
+            @pl.when(at_home)
+            def _():
+                states[block] = new
+                drain(states.at[pl.ds(0, MP - 1)], fin_r)
+
+            @pl.when(away)
+            def _():
+                remote(last, states.at[block], fin_s, fin_r, sibling).start()
+                drain(states, fin_r)
 
     write = pltpu.make_async_copy(states, out_hbm, out_s)
     write.start()
-    loads[3].wait()
+    loads[2].wait()
     scored = jnp.dot(
         states[...].reshape(ROWS, D), wctx[...], preferred_element_type=F32
     ).astype(BF16)
     summed = jnp.dot(counts[...], scored, preferred_element_type=F32)
     ctx_ref[...] = silu(summed + bias_ref[...].astype(F32)).astype(BF16)
 
-    for copy in exchange:
-        copy.wait_send()
+    gains.wait_send()
     swap.wait_send()
+    drain(w4.at[0], wex_s.at[0])
+    drain(wo.at[0], wex_s.at[1])
+    drain(nrm.at[1, pl.ds(0, MP - 1)], ag_s.at[1])
+    drain(xcols.at[pl.ds(0, MP - 1)], ag_s.at[0])
+    drain(states.at[pl.ds(0, MP - 1)], fin_s)
+    for sec in range(2):
+        drain(pairin.at[sec], pair_s.at[sec])
+        drain(pairsum.at[sec], rs_s.at[sec])
+
+    @pl.when(y != p)
+    def _():
+        drain(xcols.at[0], ag_s.at[0])
+
+    @pl.when(away)
+    def _():
+        drain(states.at[0], fin_s)
 
     @pl.when(is_even)
     def _():
@@ -308,12 +423,9 @@
     def _():
         drain(reqout, req_s)
         drain(repout, rep_s)
-
-    drain(xcols.at[pl.ds(0, MP - 1)], ag_s.at[0])
-    drain(nrm.at[1, pl.ds(0, MP - 1)], ag_s.at[1])
-    drain(states.at[pl.ds(0, MP - 1)], ag_s.at[2])
-    for sec in range(2):
-        drain(part.at[sec, pl.ds(0, MP - 1)], rs_s.at[sec])
+        drain(w4.at[0], wex_s.at[0])
+        drain(wo.at[0], wex_s.at[1])
+
     write.wait()
 
 
@@ -333,7 +445,7 @@
         in_specs=[vmem] * 6 + [hbm] * 4,
         out_specs=(hbm, vmem),
         scratch_shapes=[
-            pltpu.VMEM((D, HD), BF16),
+            pltpu.VMEM((D, 2 * HD), BF16),
             pltpu.VMEM((2, 4 * D, HD), BF16),
             pltpu.VMEM((2, D, 4 * HD), BF16),
             pltpu.VMEM((2, HD, D), BF16),
@@ -346,27 +458,38 @@
             pltpu.VMEM((2, ROWS, PEERS * SLOTS), BF16),
             pltpu.VMEM((2, ROWS, HD), BF16),
             pltpu.VMEM((ROWS, HD), BF16),
+            pltpu.VMEM((ROWS, HD), BF16),
             pltpu.VMEM((MP, ROWS, HD), BF16),
             pltpu.VMEM((ROWS, ROWS), F32),
             pltpu.VMEM((ROWS, ROWS), BF16),
             pltpu.VMEM((2, MP, OWN, D), BF16),
             pltpu.VMEM((2, MP, OWN, D), BF16),
-            pltpu.VMEM((2, MP, OWN, D), BF16),
+            pltpu.VMEM((2, 4, OWN, D), BF16),
+            pltpu.VMEM((2, 3, OWN, D), BF16),
+            pltpu.VMEM((2, 3, OWN, D), BF16),
             pltpu.VMEM((OWN, D), F32),
+            pltpu.VMEM((OWN, D), BF16),
             pltpu.VMEM((MP, OWN, D), BF16),
-            dma((4,)),
-            dma(()),
-            dma(()),
-            dma(()),
-            dma(()),
             dma((3,)),
-            dma((3,)),
-            dma(()),
-            dma(()),
-            dma((3,)),
-            dma((3,)),
+            dma(()),
+            dma(()),
+            dma(()),
+            dma(()),
             dma((2,)),
-            dma((2, MP)),
+            dma((2, 2)),
+            dma(()),
+            dma(()),
+            dma(()),
+            dma(()),
+            dma((2,)),
+            dma((MP,)),
+            dma((MP,)),
+            dma((2,)),
+            dma((2, 4)),
+            dma((2,)),
+            dma((2, 3)),
+            dma(()),
+            dma(()),
             dma(()),
         ],
         compiler_params=pltpu.CompilerParams(

time: 88.5 us -> 88.9 us (level)
  no operation moved by 1% of the time
where the time goes in v2:
time: 88.9 us; the launch traced here: 88.6 us
  Pallas kernels  84.6 us (95%)
  local copies, waits for them, and re-layouts  3.34 us (4%)
    pallas_call x1, Pallas kernels, on_device(): pl.pallas_call(kernel, out_shape=(jax.ShapeDtypeStruct((MP, OWN, D), BF16...  84.6 us
    unnamed x2, local copies, waits for them, and re-layouts  3.34 us

profile of v2, /device:TPU:1, one launch (start us, length us, event | category | flops | bytes accessed | tf_op | source)
XLA Modules:
  0.0 88.6 jit_solution(3728349915196406405)
XLA Ops:
  0.6 84.6 %cascade.1 = (bf16[8,32,1024]{2,1,0:T(8,128)(2,1)}, bf16[256,128]{1,0:T(8,128)(2,1)}) custom-call(s32[1,512]{1,0:T(1,128)} %bitcast.16, s32[1,512]{1,0:T(1,128)} %bitcast.17, s32[2,256]{1,0:T(2,128)} %bitcast.18, s32[2,8,256]{2,1,0:T(8,128)} %bitcast.15, bf16[1,1024]{1,0:T(2,128)(2,1)} %gain_ref.1, bf16[1,128]{1,0:T(2,128)(2,1)} %bitcast.19, ...), custom_call_target="tpu_custom_call" | custom-call | tf_op jit(solution)/shard_map/cascade/pallas_call | solution.py:439
  85.3 1.9 %copy.14 = bf16[1,1,256,1024]{3,2,1,0:T(8,128)(2,1)} copy(bf16[1,1,256,1024]{3,2,1,0:T(8,128)(2,1)} %bitcast.12) | data formatting | bytes 1048576
  87.1 1.5 %copy.15 = bf16[1,1,256,128]{3,2,1,0:T(8,128)(2,1)} copy(bf16[1,1,256,128]{3,2,1,0:T(8,128)(2,1)} %bitcast.14) | data formatting | bytes 131072

commit v3 on v1

--- a/solution.py
+++ b/solution.py
@@ -21,7 +21,8 @@
 YN = 4
 PEERS = ZN // 2 * YN
 SLOTS = 32
-OWN = ROWS // MP
+HALF = ROWS // 2
+OWN = HALF // MP
 EPS = 1e-06
 
 
@@ -44,7 +45,7 @@
     owner_ref, item_ref, seg_ref, nbr_ref, gain_ref, bias_ref, table_hbm, w_hbm, wo_hbm, wctx_hbm,
     out_hbm, ctx_ref,
     tcol, w4, wp, wo, wctx, gbuf, reqout, reqin, repout, repin, pick, part0, partin, xcols,
-    mask, counts, nrm, part, rsin, xrow, states,
+    mask, counts, nrm, feats, part, rsin, xrow, states,
     loc, req_s, req_r, rep_s, rep_r, wex_s, wex_r, xp_s, xp_r, ag_s, ag_r, rs_s, rs_r, out_s,
 ):
     g = lax.axis_index("dp")
@@ -171,7 +172,7 @@
                 ]
             return carry
 
-        lax.fori_loop(0, D // per_chunk, body, 0)
+        lax.fori_loop(0, D // per_chunk, body, 0, unroll=True)
 
     arrange(p)
     key_col = to_column(key)
@@ -227,72 +228,84 @@
     swap = remote(part0.at[q], partin, xp_s, xp_r, sibling)
     swap.start()
     swap.wait_recv()
-    xcols[m] = part0[p] + partin[...]
+    own = part0[p] + partin[...]
+    for h in range(2):
+        xcols[h, m] = own[h * HALF : (h + 1) * HALF]
 
     def to_group(src_of, dst, s_sem, r_of):
         for d in (4, 2, 6, 5, 7, 1, 3):
             to = mp_peer(d)
             remote(src_of(to), dst, s_sem, r_of, (g, to, p)).start()
 
-    to_group(lambda to: xcols.at[m], xcols.at[m], ag_s.at[0], ag_r.at[0])
-    drain(xcols.at[pl.ds(0, MP - 1)], ag_r.at[0])
-
-    total = jnp.zeros((ROWS, 1), F32)
-    for k in range(MP):
-        block = xcols[k].astype(F32)
-        total = total + jnp.sum(block * block, axis=1, keepdims=True)
-    inv = lax.rsqrt(total * (1.0 / D) + EPS)
-    for k in range(MP):
-        scaled = xcols[k].astype(F32) * inv * gbuf[0, 0:1, k * HD : (k + 1) * HD]
-        nrm[0, :, :, k * HD : (k + 1) * HD] = scaled.astype(BF16).reshape(MP, OWN, HD)
+    for h in range(2):
+        to_group(lambda to: xcols.at[h, m], xcols.at[h, m], ag_s.at[0], ag_r.at[0, h])
+
     own_row = pl.multiple_of(m * OWN, OWN)
-    for k in range(MP):
-        xrow[:, k * HD : (k + 1) * HD] = xcols[k, pl.ds(own_row, OWN), :].astype(F32)
-
     for sec in range(2):
-        proj = jnp.dot(
-            nrm[sec].reshape(ROWS, D), wp[sec], preferred_element_type=F32
+        for h in range(2):
+            if sec == 0:
+                drain(xcols.at[h, pl.ds(0, MP - 1)], ag_r.at[0, h])
+                total = jnp.zeros((HALF, 1), F32)
+                for k in range(MP):
+                    block = xcols[h, k].astype(F32)
+                    total = total + jnp.sum(block * block, axis=1, keepdims=True)
+                inv = lax.rsqrt(total * (1.0 / D) + EPS)
+                for k in range(MP):
+                    scaled = xcols[h, k].astype(F32) * inv * gbuf[0, 0:1, k * HD : (k + 1) * HD]
+                    nrm[0, h, :, :, k * HD : (k + 1) * HD] = scaled.astype(BF16).reshape(MP, OWN, HD)
+                    xrow[h, :, k * HD : (k + 1) * HD] = xcols[h, k, pl.ds(own_row, OWN), :].astype(F32)
+            else:
+                drain(nrm.at[1, h, pl.ds(0, MP - 1)], ag_r.at[1, h])
+            proj = jnp.dot(nrm[sec, h].reshape(HALF, D), wp[sec], preferred_element_type=F32)
+            proj = silu(proj).astype(BF16)
+            rows = slice(h * HALF, (h + 1) * HALF)
+            seen = slice(0, (h + 1) * HALF)
+            feats[rows] = proj
+            gate, query = proj[:, :HD], proj[:, 2 * HD : 3 * HD]
+            scores = lax.dot_general(
+                query, feats[seen, 3 * HD :], (((1,), (1,)), ((), ())), preferred_element_type=F32
+            ) * HD ** (-0.5)
+            attn = (silu(scores) * mask[rows, seen]).astype(BF16)
+            mixed = jnp.dot(attn, feats[seen, HD : 2 * HD], preferred_element_type=F32)
+            mixed = mixed * lax.rsqrt(jnp.mean(mixed * mixed, axis=1, keepdims=True) + EPS)
+            gated = (mixed * gate.astype(F32)).astype(BF16)
+            back = jnp.dot(gated, wo[sec], preferred_element_type=F32).astype(BF16)
+            part[sec, h] = back.reshape(MP, OWN, D)
+            to_group(
+                lambda to: part.at[sec, h, to], rsin.at[sec, h, m], rs_s.at[sec], rs_r.at[sec, h, m]
+            )
+        for h in range(2):
+            acc = xrow[h] + part[sec, h, m].astype(F32)
+            for d in (1, 3, 5, 7, 2, 6, 4):
+                src = mp_peer(d)
+                drain(rsin.at[sec, h, src], rs_r.at[sec, h, src])
+                acc = acc + rsin[sec, h, src].astype(F32)
+            new = acc.astype(BF16)
+            if sec == 0:
+                newf = new.astype(F32)
+                xrow[h] = newf
+                inv = lax.rsqrt(jnp.mean(newf * newf, axis=1, keepdims=True) + EPS)
+                nrm[1, h, m] = (newf * inv * gbuf[1, 0:1, :]).astype(BF16)
+                to_group(lambda to: nrm.at[1, h, m], nrm.at[1, h, m], ag_s.at[1], ag_r.at[1, h])
+            else:
+                states[h, m] = new
+                to_group(lambda to: states.at[h, m], states.at[h, m], ag_s.at[2], ag_r.at[2, h])
+
+    loads[3].wait()
+    writes = []
+    scored = []
+    for h in range(2):
+        drain(states.at[h, pl.ds(0, MP - 1)], ag_r.at[2, h])
+        writes.append(pltpu.make_async_copy(states.at[h], out_hbm.at[h], out_s.at[h]))
+        writes[h].start()
+        scored.append(
+            jnp.dot(
+                states[h].reshape(HALF, D), wctx[...], preferred_element_type=F32
+            ).astype(BF16)
         )
-        proj = silu(proj).astype(BF16)
-        gate, value = proj[:, :HD], proj[:, HD : 2 * HD]
-        query, keys = proj[:, 2 * HD : 3 * HD], proj[:, 3 * HD :]
-        scores = lax.dot_general(
-            query, keys, (((1,), (1,)), ((), ())), preferred_element_type=F32
-        ) * HD ** (-0.5)
-        attn = (silu(scores) * mask[...]).astype(BF16)
-        mixed = jnp.dot(attn, value, preferred_element_type=F32)
-        mixed = mixed * lax.rsqrt(jnp.mean(mixed * mixed, axis=1, keepdims=True) + EPS)
-        gated = (mixed * gate.astype(F32)).astype(BF16)
-        back = jnp.dot(gated, wo[sec], preferred_element_type=F32).astype(BF16)
-        part[sec] = back.reshape(MP, OWN, D)
-        to_group(
-            lambda to: part.at[sec, to], rsin.at[sec, m], rs_s.at[sec], rs_r.at[sec, m]
-        )
-        acc = part[sec, m].astype(F32)
-        for d in (1, 3, 5, 7, 2, 6, 4):
-            src = mp_peer(d)
-            drain(rsin.at[sec, src], rs_r.at[sec, src])
-            acc = acc + rsin[sec, src].astype(F32)
-        new = (xrow[...] + acc).astype(BF16)
-        if sec == 0:
-            newf = new.astype(F32)
-            xrow[...] = newf
-            inv = lax.rsqrt(jnp.mean(newf * newf, axis=1, keepdims=True) + EPS)
-            nrm[1, m] = (newf * inv * gbuf[1, 0:1, :]).astype(BF16)
-            to_group(lambda to: nrm.at[1, m], nrm.at[1, m], ag_s.at[1], ag_r.at[1])
-            drain(nrm.at[1, pl.ds(0, MP - 1)], ag_r.at[1])
-        else:
-            states[m] = new
-            to_group(lambda to: states.at[m], states.at[m], ag_s.at[2], ag_r.at[2])
-            drain(states.at[pl.ds(0, MP - 1)], ag_r.at[2])
-
-    write = pltpu.make_async_copy(states, out_hbm, out_s)
-    write.start()
-    loads[3].wait()
-    scored = jnp.dot(
-        states[...].reshape(ROWS, D), wctx[...], preferred_element_type=F32
-    ).astype(BF16)
-    summed = jnp.dot(counts[...], scored, preferred_element_type=F32)
+    summed = jnp.dot(
+        counts[...], jnp.concatenate(scored, axis=0), preferred_element_type=F32
+    )
     ctx_ref[...] = silu(summed + bias_ref[...].astype(F32)).astype(BF16)
 
     for copy in exchange:
@@ -309,12 +322,13 @@
         drain(reqout, req_s)
         drain(repout, rep_s)
 
-    drain(xcols.at[pl.ds(0, MP - 1)], ag_s.at[0])
-    drain(nrm.at[1, pl.ds(0, MP - 1)], ag_s.at[1])
-    drain(states.at[pl.ds(0, MP - 1)], ag_s.at[2])
-    for sec in range(2):
-        drain(part.at[sec, pl.ds(0, MP - 1)], rs_s.at[sec])
-    write.wait()
+    for h in range(2):
+        drain(xcols.at[h, pl.ds(0, MP - 1)], ag_s.at[0])
+        drain(nrm.at[1, h, pl.ds(0, MP - 1)], ag_s.at[1])
+        drain(states.at[h, pl.ds(0, MP - 1)], ag_s.at[2])
+        for sec in range(2):
+            drain(part.at[sec, h, pl.ds(0, MP - 1)], rs_s.at[sec])
+        writes[h].wait()
 
 
 def on_device(
@@ -327,7 +341,7 @@
     states, ctx = pl.pallas_call(
         kernel,
         out_shape=(
-            jax.ShapeDtypeStruct((MP, OWN, D), BF16),
+            jax.ShapeDtypeStruct((2, MP, OWN, D), BF16),
             jax.ShapeDtypeStruct((ROWS, HD), BF16),
         ),
         in_specs=[vmem] * 6 + [hbm] * 4,
@@ -346,14 +360,15 @@
             pltpu.VMEM((2, ROWS, PEERS * SLOTS), BF16),
             pltpu.VMEM((2, ROWS, HD), BF16),
             pltpu.VMEM((ROWS, HD), BF16),
-            pltpu.VMEM((MP, ROWS, HD), BF16),
+            pltpu.VMEM((2, MP, HALF, HD), BF16),
             pltpu.VMEM((ROWS, ROWS), F32),
             pltpu.VMEM((ROWS, ROWS), BF16),
+            pltpu.VMEM((2, 2, MP, OWN, D), BF16),
+            pltpu.VMEM((ROWS, 4 * HD), BF16),
+            pltpu.VMEM((2, 2, MP, OWN, D), BF16),
+            pltpu.VMEM((2, 2, MP, OWN, D), BF16),
+            pltpu.VMEM((2, OWN, D), F32),
             pltpu.VMEM((2, MP, OWN, D), BF16),
-            pltpu.VMEM((2, MP, OWN, D), BF16),
-            pltpu.VMEM((2, MP, OWN, D), BF16),
-            pltpu.VMEM((OWN, D), F32),
-            pltpu.VMEM((MP, OWN, D), BF16),
             dma((4,)),
             dma(()),
             dma(()),
@@ -364,10 +379,10 @@
             dma(()),
             dma(()),
             dma((3,)),
-            dma((3,)),
+            dma((3, 2)),
             dma((2,)),
-            dma((2, MP)),
-            dma(()),
+            dma((2, 2, MP)),
+            dma((2,)),
         ],
         compiler_params=pltpu.CompilerParams(
             collective_id=0, has_side_effects=True, vmem_limit_bytes=60 * 1024 * 1024

time: 88.5 us -> 80.1 us (0.905)
  Pallas kernels: 84.3 us -> 75.8 us
    pallas_call x1, Pallas kernels: 84.3 us -> 75.8 us  [on_device(): pl.pallas_call(kernel, out_shape=(jax.ShapeDtypeStruct((2, MP, OWN, D), B...]
where the time goes in v3:
time: 80.1 us; the launch traced here: 79.8 us
  Pallas kernels  75.8 us (95%)
  local copies, waits for them, and re-layouts  3.34 us (4%)
    pallas_call x1, Pallas kernels, on_device(): pl.pallas_call(kernel, out_shape=(jax.ShapeDtypeStruct((2, MP, OWN, D), B...  75.8 us
    unnamed x2, local copies, waits for them, and re-layouts  3.34 us

profile of v3, /device:TPU:1, one launch (start us, length us, event | category | flops | bytes accessed | tf_op | source)
XLA Modules:
  0.0 79.8 jit_solution(5866515350423108397)
XLA Ops:
  0.6 75.8 %cascade.1 = (bf16[2,8,16,1024]{3,2,1,0:T(8,128)(2,1)}, bf16[256,128]{1,0:T(8,128)(2,1)}) custom-call(s32[1,512]{1,0:T(1,128)} %bitcast.16, s32[1,512]{1,0:T(1,128)} %bitcast.17, s32[2,256]{1,0:T(2,128)} %bitcast.18, s32[2,8,256]{2,1,0:T(8,128)} %bitcast.15, bf16[1,1024]{1,0:T(2,128)(2,1)} %gain_ref.1, bf16[1,128]{1,0:T(2,128)(2,1)} %bitcast.19, ...), custom_call_target="tpu_custom_call" | custom-call | tf_op jit(solution)/shard_map/cascade/pallas_call | solution.py:341
  76.4 1.9 %copy.14 = bf16[1,1,256,1024]{3,2,1,0:T(8,128)(2,1)} copy(bf16[1,1,256,1024]{3,2,1,0:T(8,128)(2,1)} %bitcast.12) | data formatting | bytes 1048576
  78.3 1.5 %copy.15 = bf16[1,1,256,128]{3,2,1,0:T(8,128)(2,1)} copy(bf16[1,1,256,128]{3,2,1,0:T(8,128)(2,1)} %bitcast.14) | data formatting | bytes 131072

commit v4 on v3

--- a/solution.py
+++ b/solution.py
@@ -20,7 +20,7 @@
 ZN = 12
 YN = 4
 PEERS = ZN // 2 * YN
-SLOTS = 32
+SLOTS = 24
 HALF = ROWS // 2
 OWN = HALF // MP
 EPS = 1e-06
@@ -42,11 +42,11 @@
 
 
 def kernel(
-    owner_ref, item_ref, seg_ref, nbr_ref, gain_ref, bias_ref, table_hbm, w_hbm, wo_hbm, wctx_hbm,
-    out_hbm, ctx_ref,
-    tcol, w4, wp, wo, wctx, gbuf, reqout, reqin, repout, repin, pick, part0, partin, xcols,
-    mask, counts, nrm, feats, part, rsin, xrow, states,
-    loc, req_s, req_r, rep_s, rep_r, wex_s, wex_r, xp_s, xp_r, ag_s, ag_r, rs_s, rs_r, out_s,
+    owner_ref, item_ref, seg_ref, nbr_ref, gain_ref, table_hbm, w_hbm, wo_hbm, wctx_hbm,
+    states, counts, wctx,
+    tcol, w4, wp, wo, gbuf, reqout, reqin, repout, repin, pick, part0, partin, xcols,
+    mask, nrm, feats, part, rsin, xrow,
+    loc, req_s, req_r, rep_s, rep_r, wex_s, wex_r, xp_s, xp_r, ag_s, ag_r, rs_s, rs_r,
 ):
     g = lax.axis_index("dp")
     m = lax.axis_index("mp")
@@ -96,8 +96,9 @@
         pltpu.make_async_copy(table_hbm.at[:, pl.ds(col0, HD)], tcol, loc.at[0]),
         pltpu.make_async_copy(w_hbm, w4.at[p], loc.at[1]),
         pltpu.make_async_copy(wo_hbm, wo.at[p], loc.at[2]),
-        pltpu.make_async_copy(wctx_hbm, wctx, loc.at[3]),
     ]
+    keep = pltpu.make_async_copy(wctx_hbm, wctx, loc.at[3])
+    keep.start()
     for load in loads:
         load.start()
     gbuf[p] = jnp.broadcast_to(gain_ref[...].astype(F32), (8, D))
@@ -219,6 +220,7 @@
         row = jnp.broadcast_to(near[n : n + 1], (ROWS, ROWS))
         hits = hits + jnp.where(row == iota((ROWS, ROWS), 0), 1.0 / NBR, 0.0)
     counts[...] = hits.T.astype(BF16)
+    keep.wait()
 
     drain(repin, rep_r)
     for h in range(2):
@@ -291,22 +293,8 @@
                 states[h, m] = new
                 to_group(lambda to: states.at[h, m], states.at[h, m], ag_s.at[2], ag_r.at[2, h])
 
-    loads[3].wait()
-    writes = []
-    scored = []
     for h in range(2):
         drain(states.at[h, pl.ds(0, MP - 1)], ag_r.at[2, h])
-        writes.append(pltpu.make_async_copy(states.at[h], out_hbm.at[h], out_s.at[h]))
-        writes[h].start()
-        scored.append(
-            jnp.dot(
-                states[h].reshape(HALF, D), wctx[...], preferred_element_type=F32
-            ).astype(BF16)
-        )
-    summed = jnp.dot(
-        counts[...], jnp.concatenate(scored, axis=0), preferred_element_type=F32
-    )
-    ctx_ref[...] = silu(summed + bias_ref[...].astype(F32)).astype(BF16)
 
     for copy in exchange:
         copy.wait_send()
@@ -328,7 +316,17 @@
         drain(states.at[h, pl.ds(0, MP - 1)], ag_s.at[2])
         for sec in range(2):
             drain(part.at[sec, h, pl.ds(0, MP - 1)], rs_s.at[sec])
-        writes[h].wait()
+
+
+def finish(states_ref, counts_ref, wctx_ref, bias_ref, out_hbm, ctx_ref, sem):
+    write = pltpu.make_async_copy(states_ref, out_hbm, sem)
+    write.start()
+    scored = jnp.dot(
+        states_ref[...].reshape(ROWS, D), wctx_ref[...], preferred_element_type=F32
+    ).astype(BF16)
+    summed = jnp.dot(counts_ref[...], scored, preferred_element_type=F32)
+    ctx_ref[...] = silu(summed + bias_ref[...].astype(F32)).astype(BF16)
+    write.wait()
 
 
 def on_device(
@@ -336,22 +334,22 @@
 ):
     n_rows = item_row.shape[0]
     vmem = pl.BlockSpec(memory_space=pltpu.VMEM)
-    hbm = pl.BlockSpec(memory_space=pl.ANY)
+    hbm = pl.BlockSpec(memory_space=pltpu.HBM)
     dma = pltpu.SemaphoreType.DMA
-    states, ctx = pl.pallas_call(
+    states, counts, wctx = pl.pallas_call(
         kernel,
         out_shape=(
-            jax.ShapeDtypeStruct((2, MP, OWN, D), BF16),
-            jax.ShapeDtypeStruct((ROWS, HD), BF16),
+            pltpu.VMEM((2, MP, OWN, D), BF16),
+            pltpu.VMEM((ROWS, ROWS), BF16),
+            pltpu.VMEM((D, HD), BF16),
         ),
-        in_specs=[vmem] * 6 + [hbm] * 4,
-        out_specs=(hbm, vmem),
+        in_specs=[vmem] * 5 + [hbm] * 4,
+        out_specs=(vmem, vmem, vmem),
         scratch_shapes=[
             pltpu.VMEM((D, HD), BF16),
             pltpu.VMEM((2, 4 * D, HD), BF16),
             pltpu.VMEM((2, D, 4 * HD), BF16),
             pltpu.VMEM((2, HD, D), BF16),
-            pltpu.VMEM((D, HD), BF16),
             pltpu.VMEM((2, 8, D), F32),
             pltpu.VMEM((PEERS, 1, HD), I32),
             pltpu.VMEM((PEERS, 1, HD), I32),
@@ -362,13 +360,11 @@
             pltpu.VMEM((ROWS, HD), BF16),
             pltpu.VMEM((2, MP, HALF, HD), BF16),
             pltpu.VMEM((ROWS, ROWS), F32),
-            pltpu.VMEM((ROWS, ROWS), BF16),
             pltpu.VMEM((2, 2, MP, OWN, D), BF16),
             pltpu.VMEM((ROWS, 4 * HD), BF16),
             pltpu.VMEM((2, 2, MP, OWN, D), BF16),
             pltpu.VMEM((2, 2, MP, OWN, D), BF16),
             pltpu.VMEM((2, OWN, D), F32),
-            pltpu.VMEM((2, MP, OWN, D), BF16),
             dma((4,)),
             dma(()),
             dma(()),
@@ -382,10 +378,9 @@
             dma((3, 2)),
             dma((2,)),
             dma((2, 2, MP)),
-            dma((2,)),
         ],
         compiler_params=pltpu.CompilerParams(
-            collective_id=0, has_side_effects=True, vmem_limit_bytes=60 * 1024 * 1024
+            collective_id=0, has_side_effects=True, vmem_limit_bytes=65700000
         ),
         name="cascade",
     )(
@@ -394,12 +389,23 @@
         segments[0],
         jnp.swapaxes(neighbors[0], 1, 2),
         gains,
-        ctx_bias.reshape(1, -1),
         table,
         w_in.reshape(4 * D, HD),
         w_out[0],
         w_ctx,
     )
+    states, ctx = pl.pallas_call(
+        finish,
+        out_shape=(
+            jax.ShapeDtypeStruct((2, MP, OWN, D), BF16),
+            jax.ShapeDtypeStruct((ROWS, HD), BF16),
+        ),
+        in_specs=[vmem] * 4,
+        out_specs=(hbm, vmem),
+        scratch_shapes=[dma(())],
+        compiler_params=pltpu.CompilerParams(vmem_limit_bytes=8 * 1024 * 1024),
+        name="finish",
+    )(states, counts, wctx, ctx_bias.reshape(1, -1))
     return states.reshape(1, 1, ROWS, D), ctx.reshape(1, 1, ROWS, HD)
 
 

time: 80.1 us -> 75.3 us (0.940)
  local copies, waits for them, and re-layouts: 3.34 us -> 0.01 us
  Pallas kernels: 75.8 us -> 74.4 us
    unnamed x2, local copies, waits for them, and re-layouts: 3.34 us -> 0.01 us
    pallas_call x1 -> x2, Pallas kernels: 75.8 us -> 74.4 us  [the longest x1 72.9 us: on_device(): pl.pallas_call(kernel, out_shape=(pltpu.VMEM((2, MP, OWN, D), BF16), pltp...]
where the time goes in v4:
time: 75.3 us; the launch traced here: 75.1 us
  Pallas kernels  74.4 us (99%)
    pallas_call x1, Pallas kernels, on_device(): pl.pallas_call(kernel, out_shape=(pltpu.VMEM((2, MP, OWN, D), BF16), pltp...  72.9 us
    pallas_call x1, Pallas kernels, on_device(): pl.pallas_call(finish, out_shape=(jax.ShapeDtypeStruct((2, MP, OWN, D), B...  1.51 us

profile of v4, /device:TPU:1, one launch (start us, length us, event | category | flops | bytes accessed | tf_op | source)
XLA Modules:
  0.0 75.1 jit_solution(2703411604463309464)
XLA Ops:
  0.6 0.0 copy-start
  0.6 72.9 %cascade.1 = (bf16[2,8,16,1024]{3,2,1,0:T(8,128)(2,1)S(1)}, bf16[256,256]{1,0:T(8,128)(2,1)S(1)}, bf16[1024,128]{1,0:T(8,128)(2,1)S(1)}) custom-call(s32[1,512]{1,0:T(1,128)} %bitcast.15, s32[1,512]{1,0:T(1,128)} %bitcast.16, s32[2,256]{1,0:T(2,128)} %bitcast.17, s32[2,8,256]{2,1,0:T(8,128)} %bitcast.14, bf16[1,1024]{1,0:T(2,128)(2,1)} %gain_ref.1, ...), custom_call_target="tpu_custom_call" | custom-call | tf_op jit(solution)/shard_map/cascade/pallas_call | solution.py:339
  73.6 0.0 copy-done
  73.6 1.5 %finish.1 = (bf16[2,8,16,1024]{3,2,1,0:T(8,128)(2,1)}, bf16[256,128]{1,0:T(8,128)(2,1)}) custom-call(bf16[2,8,16,1024]{3,2,1,0:T(8,128)(2,1)S(1)} %get-tuple-element.7.states_ref, bf16[256,256]{1,0:T(8,128)(2,1)S(1)} %get-tuple-element.8.counts_ref, bf16[1024,128]{1,0:T(8,128)(2,1)S(1)} %get-tuple-element.9.wctx_ref, bf16[1,128]{1,0:T(2,128)(2,1)S(1)} %bitcast.11), custom_call_target="tpu_custom_call" | custom-call | tf_op jit(solution)/shard_map/finish/pallas_call | solution.py:397
Async XLA Ops:
  0.6 72.9 %copy-start = (bf16[128]{0:T(256)(128)(2,1)S(1)}, bf16[128]{0:T(256)(128)(2,1)}, u32[]{:S(2)}) copy-start(bf16[128]{0:T(256)(128)(2,1)} %param.19) | copy-start | bytes 772

commit v5 on v4

--- a/solution.py
+++ b/solution.py
@@ -56,10 +56,12 @@
     slot_me = (zg // 2) * YN + yg
     is_even = p == 0
 
+    m_y = lax.rem(m + MP // 2, MP)
+
     def dp_peer(j, dy):
         z = lax.rem(zg + 2 * j + p, ZN)
         y = lax.rem(yg + dy, YN)
-        return z * YN + y, (z // 2) * YN + y
+        return (z * YN + y, m_y if dy == 2 else m, p), (z // 2) * YN + y
 
     def mp_peer(d):
         return lax.rem(m + d, MP)
@@ -80,22 +82,24 @@
     far_first = (3, 2, 4, 1, 5, 0)
     for j in far_first:
         for dy in (2, 1, 3, 0):
-            o, _ = dp_peer(j, dy)
+            dev, _ = dp_peer(j, dy)
             if (j, dy) == (0, 0):
                 @pl.when(p == 1)
                 def _():
-                    greet((o, m, p))
+                    greet(dev)
             else:
-                greet((o, m, p))
+                greet(dev)
     for d in range(1, MP):
         greet((g, mp_peer(d), p))
     greet((g, m, q))
 
     col0 = pl.multiple_of(m * HD, HD)
+    col1 = pl.multiple_of(m_y * HD, HD)
     loads = [
-        pltpu.make_async_copy(table_hbm.at[:, pl.ds(col0, HD)], tcol, loc.at[0]),
+        pltpu.make_async_copy(table_hbm.at[:, pl.ds(col0, HD)], tcol.at[:, :HD], loc.at[0]),
         pltpu.make_async_copy(w_hbm, w4.at[p], loc.at[1]),
         pltpu.make_async_copy(wo_hbm, wo.at[p], loc.at[2]),
+        pltpu.make_async_copy(table_hbm.at[:, pl.ds(col1, HD)], tcol.at[:, HD:], loc.at[4]),
     ]
     keep = pltpu.make_async_copy(wctx_hbm, wctx, loc.at[3])
     keep.start()
@@ -130,18 +134,28 @@
 
     def to_peers(src_of, dst, s_sem, r_sem, js):
         for j in js:
+            seen_as = lax.rem(ZN // 2 - j - p, ZN // 2)
             for dy in (2, 1, 3, 0):
-                o, s = dp_peer(j, dy)
+                dev, s = dp_peer(j, dy)
                 if (j, dy) == (0, 0):
                     @pl.when(is_even)
                     def _():
-                        pltpu.make_async_copy(src_of.at[s], dst.at[slot_me], r_sem).start()
+                        pltpu.make_async_copy(
+                            src_of.at[s], dst.at[slot_me], r_sem.at[seen_as]
+                        ).start()
 
                     @pl.when(p == 1)
                     def _():
-                        remote(src_of.at[s], dst.at[slot_me], s_sem, r_sem, (o, m, p)).start()
+                        remote(
+                            src_of.at[s], dst.at[slot_me], s_sem, r_sem.at[seen_as], dev
+                        ).start()
                 else:
-                    remote(src_of.at[s], dst.at[slot_me], s_sem, r_sem, (o, m, p)).start()
+                    remote(
+                        src_of.at[s], dst.at[slot_me], s_sem, r_sem.at[seen_as], dev
+                    ).start()
+
+    def peers_at(j):
+        return pl.ds((lax.rem(zg + 2 * j + p, ZN) // 2) * YN, YN)
 
     to_peers(reqout, reqin, req_s, req_r, far_first)
 
@@ -176,19 +190,14 @@
         lax.fori_loop(0, D // per_chunk, body, 0, unroll=True)
 
     arrange(p)
-    key_col = to_column(key)
-    for h in range(2):
-        lanes = iota((ROWS, PEERS * SLOTS), 1).astype(F32)
-        pick[h] = (key_col[h * ROWS : (h + 1) * ROWS] == lanes).astype(F32).astype(BF16)
-
     loads[0].wait()
-    drain(reqin, req_r)
-    for pair in ((3, 2), (4, 1), (5, 0)):
+    loads[3].wait()
+    crossed = lax.rem(yg + 2, YN)
+    for pair in ((0, 5), (1, 4), (2, 3)):
         columns = []
         for j in pair:
-            z = lax.rem(zg + 2 * j + p, ZN)
-            base = (z // 2) * YN
-            asked = jnp.broadcast_to(reqin[pl.ds(base, YN)], (YN, SLOTS, HD))
+            drain(reqin.at[peers_at(j)], req_r.at[j])
+            asked = jnp.broadcast_to(reqin[peers_at(j)], (YN, SLOTS, HD))
             on = iota((YN, SLOTS, HD), 1) == iota((YN, SLOTS, HD), 2)
             columns.append(
                 jnp.sum(jnp.where(on, asked.astype(F32), 0.0), axis=2, keepdims=True).reshape(
@@ -198,12 +207,18 @@
         column = jnp.concatenate(columns, axis=0)
         size = 2 * YN * SLOTS
         hot = (column == iota((size, D), 1).astype(F32)).astype(F32).astype(BF16)
-        rows = jnp.dot(hot, tcol[...], preferred_element_type=F32).astype(BF16)
+        rows = jnp.dot(hot, tcol[...], preferred_element_type=F32)
+        group = (iota((size, HD), 0) // SLOTS) % YN
+        rows = jnp.where(group == crossed, rows[:, HD:], rows[:, :HD]).astype(BF16)
         rows = rows.reshape(2, YN, SLOTS, HD)
         for i, j in enumerate(pair):
-            z = lax.rem(zg + 2 * j + p, ZN)
-            repout[pl.ds((z // 2) * YN, YN)] = rows[i]
-        to_peers(repout, repin, rep_s, rep_r, pair)
+            repout[peers_at(j)] = rows[i]
+        to_peers(repout, repin, rep_s, rep_r, pair[::-1])
+
+    key_col = to_column(key)
+    for h in range(2):
+        lanes = iota((ROWS, PEERS * SLOTS), 1).astype(F32)
+        pick[h] = (key_col[h * ROWS : (h + 1) * ROWS] == lanes).astype(F32).astype(BF16)
 
     exchange[0].wait_recv()
     exchange[1].wait_recv()
@@ -222,7 +237,8 @@
     counts[...] = hits.T.astype(BF16)
     keep.wait()
 
-    drain(repin, rep_r)
+    for j in range(ZN // 2):
+        drain(repin.at[peers_at(j)], rep_r.at[j])
     for h in range(2):
         part0[h] = jnp.dot(
             pick[h], repin[...].reshape(PEERS * SLOTS, HD), preferred_element_type=F32
@@ -346,7 +362,7 @@
         in_specs=[vmem] * 5 + [hbm] * 4,
         out_specs=(vmem, vmem, vmem),
         scratch_shapes=[
-            pltpu.VMEM((D, HD), BF16),
+            pltpu.VMEM((D, 2 * HD), BF16),
             pltpu.VMEM((2, 4 * D, HD), BF16),
             pltpu.VMEM((2, D, 4 * HD), BF16),
             pltpu.VMEM((2, HD, D), BF16),
@@ -365,11 +381,11 @@
             pltpu.VMEM((2, 2, MP, OWN, D), BF16),
             pltpu.VMEM((2, 2, MP, OWN, D), BF16),
             pltpu.VMEM((2, OWN, D), F32),
-            dma((4,)),
+            dma((5,)),
             dma(()),
+            dma((ZN // 2,)),
             dma(()),
-            dma(()),
-            dma(()),
+            dma((ZN // 2,)),
             dma((3,)),
             dma((3,)),
             dma(()),

time: 75.3 us -> 74.6 us (level)
  Pallas kernels: 74.4 us -> 73.3 us
    pallas_call x1, Pallas kernels: 72.9 us -> 71.8 us  [on_device(): pl.pallas_call(kernel, out_shape=(pltpu.VMEM((2, MP, OWN, D), BF16), pltp...]
where the time goes in v5:
time: 74.6 us; the launch traced here: 74 us
  Pallas kernels  73.3 us (98%)
    pallas_call x1, Pallas kernels, on_device(): pl.pallas_call(kernel, out_shape=(pltpu.VMEM((2, MP, OWN, D), BF16), pltp...  71.8 us
    pallas_call x1, Pallas kernels, on_device(): pl.pallas_call(finish, out_shape=(jax.ShapeDtypeStruct((2, MP, OWN, D), B...  1.51 us

profile of v5, /device:TPU:1, one launch (start us, length us, event | category | flops | bytes accessed | tf_op | source)
XLA Modules:
  0.0 74.0 jit_solution(1450963205200643523)
XLA Ops:
  0.6 0.0 copy-start
  0.6 71.8 %cascade.1 = (bf16[2,8,16,1024]{3,2,1,0:T(8,128)(2,1)S(1)}, bf16[256,256]{1,0:T(8,128)(2,1)S(1)}, bf16[1024,128]{1,0:T(8,128)(2,1)S(1)}) custom-call(s32[1,512]{1,0:T(1,128)} %bitcast.15, s32[1,512]{1,0:T(1,128)} %bitcast.16, s32[2,256]{1,0:T(2,128)} %bitcast.17, s32[2,8,256]{2,1,0:T(8,128)} %bitcast.14, bf16[1,1024]{1,0:T(2,128)(2,1)} %gain_ref.1, ...), custom_call_target="tpu_custom_call" | custom-call | tf_op jit(solution)/shard_map/cascade/pallas_call | solution.py:355
  72.5 0.0 copy-done
  72.5 1.5 %finish.1 = (bf16[2,8,16,1024]{3,2,1,0:T(8,128)(2,1)}, bf16[256,128]{1,0:T(8,128)(2,1)}) custom-call(bf16[2,8,16,1024]{3,2,1,0:T(8,128)(2,1)S(1)} %get-tuple-element.7.states_ref, bf16[256,256]{1,0:T(8,128)(2,1)S(1)} %get-tuple-element.8.counts_ref, bf16[1024,128]{1,0:T(8,128)(2,1)S(1)} %get-tuple-element.9.wctx_ref, bf16[1,128]{1,0:T(2,128)(2,1)S(1)} %bitcast.11), custom_call_target="tpu_custom_call" | custom-call | tf_op jit(solution)/shard_map/finish/pallas_call | solution.py:413
Async XLA Ops:
  0.6 71.9 %copy-start = (bf16[128]{0:T(256)(128)(2,1)S(1)}, bf16[128]{0:T(256)(128)(2,1)}, u32[]{:S(2)}) copy-start(bf16[128]{0:T(256)(128)(2,1)} %param.19) | copy-start | bytes 772

commit v6 on v5

--- a/solution.py
+++ b/solution.py
@@ -20,7 +20,7 @@
 ZN = 12
 YN = 4
 PEERS = ZN // 2 * YN
-SLOTS = 24
+SLOTS = 18
 HALF = ROWS // 2
 OWN = HALF // MP
 EPS = 1e-06
@@ -42,8 +42,9 @@
 
 
 def kernel(
-    owner_ref, item_ref, seg_ref, nbr_ref, gain_ref, table_hbm, w_hbm, wo_hbm, wctx_hbm,
+    owner_hbm, item_hbm, seg_hbm, nbr_hbm, gain_hbm, table_hbm, w_hbm, wo_hbm, wctx_hbm,
     states, counts, wctx,
+    owner_ref, item_ref, seg_ref, nbr_ref, gain_ref,
     tcol, w4, wp, wo, gbuf, reqout, reqin, repout, repin, pick, part0, partin, xcols,
     mask, nrm, feats, part, rsin, xrow,
     loc, req_s, req_r, rep_s, rep_r, wex_s, wex_r, xp_s, xp_r, ag_s, ag_r, rs_s, rs_r,
@@ -101,10 +102,21 @@
         pltpu.make_async_copy(wo_hbm, wo.at[p], loc.at[2]),
         pltpu.make_async_copy(table_hbm.at[:, pl.ds(col1, HD)], tcol.at[:, HD:], loc.at[4]),
     ]
+    small = [
+        pltpu.make_async_copy(owner_hbm, owner_ref, loc.at[5]),
+        pltpu.make_async_copy(item_hbm, item_ref, loc.at[6]),
+        pltpu.make_async_copy(gain_hbm, gain_ref, loc.at[7]),
+        pltpu.make_async_copy(seg_hbm, seg_ref, loc.at[8]),
+        pltpu.make_async_copy(nbr_hbm, nbr_ref, loc.at[9]),
+    ]
+    for load in small:
+        load.start()
     keep = pltpu.make_async_copy(wctx_hbm, wctx, loc.at[3])
     keep.start()
     for load in loads:
         load.start()
+    for load in small[:3]:
+        load.wait()
     gbuf[p] = jnp.broadcast_to(gain_ref[...].astype(F32), (8, D))
 
     n_rows = owner_ref.shape[1]
@@ -197,20 +209,17 @@
         columns = []
         for j in pair:
             drain(reqin.at[peers_at(j)], req_r.at[j])
-            asked = jnp.broadcast_to(reqin[peers_at(j)], (YN, SLOTS, HD))
-            on = iota((YN, SLOTS, HD), 1) == iota((YN, SLOTS, HD), 2)
-            columns.append(
-                jnp.sum(jnp.where(on, asked.astype(F32), 0.0), axis=2, keepdims=True).reshape(
-                    YN * SLOTS, 1
-                )
-            )
+            asked = jnp.broadcast_to(reqin[peers_at(j)], (YN, 24, HD))
+            on = iota((YN, 24, HD), 1) == iota((YN, 24, HD), 2)
+            found = jnp.sum(jnp.where(on, asked.astype(F32), 0.0), axis=2, keepdims=True)
+            columns.append(found[:, :SLOTS].reshape(YN * SLOTS, 1))
         column = jnp.concatenate(columns, axis=0)
         size = 2 * YN * SLOTS
         hot = (column == iota((size, D), 1).astype(F32)).astype(F32).astype(BF16)
         rows = jnp.dot(hot, tcol[...], preferred_element_type=F32)
         group = (iota((size, HD), 0) // SLOTS) % YN
         rows = jnp.where(group == crossed, rows[:, HD:], rows[:, :HD]).astype(BF16)
-        rows = rows.reshape(2, YN, SLOTS, HD)
+        rows = rows.reshape(2, YN, SLOTS // 2, 2, HD)
         for i, j in enumerate(pair):
             repout[peers_at(j)] = rows[i]
         to_peers(repout, repin, rep_s, rep_r, pair[::-1])
@@ -224,6 +233,8 @@
     exchange[1].wait_recv()
     exchange[2].wait_recv()
     arrange(q)
+    small[3].wait()
+    small[4].wait()
     seg = seg_ref[pl.ds(p, 1), :].astype(F32)
     seg_col = to_column(seg)
     below = iota((ROWS, ROWS), 1) <= iota((ROWS, ROWS), 0)
@@ -239,23 +250,26 @@
 
     for j in range(ZN // 2):
         drain(repin.at[peers_at(j)], rep_r.at[j])
-    for h in range(2):
-        part0[h] = jnp.dot(
-            pick[h], repin[...].reshape(PEERS * SLOTS, HD), preferred_element_type=F32
-        ).astype(BF16)
-    swap = remote(part0.at[q], partin, xp_s, xp_r, sibling)
-    swap.start()
-    swap.wait_recv()
-    own = part0[p] + partin[...]
-    for h in range(2):
-        xcols[h, m] = own[h * HALF : (h + 1) * HALF]
-
     def to_group(src_of, dst, s_sem, r_of):
         for d in (4, 2, 6, 5, 7, 1, 3):
             to = mp_peer(d)
             remote(src_of(to), dst, s_sem, r_of, (g, to, p)).start()
 
+    halves = [slice(0, HALF), slice(HALF, ROWS)]
+    rows = repin[...].reshape(PEERS * SLOTS, HD)
+    swaps = []
     for h in range(2):
+        theirs = jnp.dot(pick[q, halves[h]], rows, preferred_element_type=F32)
+        part0[h] = theirs.astype(BF16)
+        swaps.append(remote(part0.at[h], partin.at[h], xp_s.at[h], xp_r.at[h], sibling))
+        swaps[h].start()
+    mine = [
+        jnp.dot(pick[p, halves[h]], rows, preferred_element_type=F32).astype(BF16)
+        for h in range(2)
+    ]
+    for h in range(2):
+        swaps[h].wait_recv()
+        xcols[h, m] = mine[h] + partin[h]
         to_group(lambda to: xcols.at[h, m], xcols.at[h, m], ag_s.at[0], ag_r.at[0, h])
 
     own_row = pl.multiple_of(m * OWN, OWN)
@@ -314,7 +328,8 @@
 
     for copy in exchange:
         copy.wait_send()
-    swap.wait_send()
+    for swap in swaps:
+        swap.wait_send()
 
     @pl.when(is_even)
     def _():
@@ -359,9 +374,14 @@
             pltpu.VMEM((ROWS, ROWS), BF16),
             pltpu.VMEM((D, HD), BF16),
         ),
-        in_specs=[vmem] * 5 + [hbm] * 4,
+        in_specs=[hbm] * 9,
         out_specs=(vmem, vmem, vmem),
         scratch_shapes=[
+            pltpu.VMEM((1, n_rows), I32),
+            pltpu.VMEM((1, n_rows), I32),
+            pltpu.VMEM((2, ROWS), I32),
+            pltpu.VMEM((2, NBR, ROWS), I32),
+            pltpu.VMEM((1, D), BF16),
             pltpu.VMEM((D, 2 * HD), BF16),
             pltpu.VMEM((2, 4 * D, HD), BF16),
             pltpu.VMEM((2, D, 4 * HD), BF16),
@@ -369,11 +389,11 @@
             pltpu.VMEM((2, 8, D), F32),
             pltpu.VMEM((PEERS, 1, HD), I32),
             pltpu.VMEM((PEERS, 1, HD), I32),
-            pltpu.VMEM((PEERS, SLOTS, HD), BF16),
-            pltpu.VMEM((PEERS, SLOTS, HD), BF16),
+            pltpu.VMEM((PEERS, SLOTS // 2, 2, HD), BF16),
+            pltpu.VMEM((PEERS, SLOTS // 2, 2, HD), BF16),
             pltpu.VMEM((2, ROWS, PEERS * SLOTS), BF16),
-            pltpu.VMEM((2, ROWS, HD), BF16),
-            pltpu.VMEM((ROWS, HD), BF16),
+            pltpu.VMEM((2, HALF, HD), BF16),
+            pltpu.VMEM((2, HALF, HD), BF16),
             pltpu.VMEM((2, MP, HALF, HD), BF16),
             pltpu.VMEM((ROWS, ROWS), F32),
             pltpu.VMEM((2, 2, MP, OWN, D), BF16),
@@ -381,15 +401,15 @@
             pltpu.VMEM((2, 2, MP, OWN, D), BF16),
             pltpu.VMEM((2, 2, MP, OWN, D), BF16),
             pltpu.VMEM((2, OWN, D), F32),
-            dma((5,)),
+            dma((10,)),
             dma(()),
             dma((ZN // 2,)),
             dma(()),
             dma((ZN // 2,)),
             dma((3,)),
             dma((3,)),
-            dma(()),
-            dma(()),
+            dma((2,)),
+            dma((2,)),
             dma((3,)),
             dma((3, 2)),
             dma((2,)),

time: 74.6 us -> 73.4 us (0.984)
  Pallas kernels: 73.3 us -> 71.9 us
    pallas_call x1, Pallas kernels: 71.8 us -> 70.4 us  [on_device(): pl.pallas_call(kernel, out_shape=(pltpu.VMEM((2, MP, OWN, D), BF16), pltp...]
where the time goes in v6:
time: 73.4 us; the launch traced here: 72.6 us
  Pallas kernels  71.9 us (98%)
    pallas_call x1, Pallas kernels, on_device(): pl.pallas_call(kernel, out_shape=(pltpu.VMEM((2, MP, OWN, D), BF16), pltp...  70.4 us
    pallas_call x1, Pallas kernels, on_device(): pl.pallas_call(finish, out_shape=(jax.ShapeDtypeStruct((2, MP, OWN, D), B...  1.51 us

profile of v6, /device:TPU:1, one launch (start us, length us, event | category | flops | bytes accessed | tf_op | source)
XLA Modules:
  0.0 72.6 jit_solution(809557846625389935)
XLA Ops:
  0.6 0.0 copy-start
  0.6 70.4 %cascade.1 = (bf16[2,8,16,1024]{3,2,1,0:T(8,128)(2,1)S(1)}, bf16[256,256]{1,0:T(8,128)(2,1)S(1)}, bf16[1024,128]{1,0:T(8,128)(2,1)S(1)}) custom-call(s32[1,512]{1,0:T(1,128)} %bitcast.15, s32[1,512]{1,0:T(1,128)} %bitcast.16, s32[2,256]{1,0:T(2,128)} %bitcast.17, s32[2,8,256]{2,1,0:T(8,128)} %bitcast.14, bf16[1,1024]{1,0:T(2,128)(2,1)} %gain_hbm.1, ...), custom_call_target="tpu_custom_call" | custom-call | tf_op jit(solution)/shard_map/cascade/pallas_call | solution.py:370
  71.1 0.0 copy-done
  71.1 1.5 %finish.1 = (bf16[2,8,16,1024]{3,2,1,0:T(8,128)(2,1)}, bf16[256,128]{1,0:T(8,128)(2,1)}) custom-call(bf16[2,8,16,1024]{3,2,1,0:T(8,128)(2,1)S(1)} %get-tuple-element.7.states_ref, bf16[256,256]{1,0:T(8,128)(2,1)S(1)} %get-tuple-element.8.counts_ref, bf16[1024,128]{1,0:T(8,128)(2,1)S(1)} %get-tuple-element.9.wctx_ref, bf16[1,128]{1,0:T(2,128)(2,1)S(1)} %bitcast.11), custom_call_target="tpu_custom_call" | custom-call | tf_op jit(solution)/shard_map/finish/pallas_call | solution.py:433
Async XLA Ops:
  0.6 70.5 %copy-start = (bf16[128]{0:T(256)(128)(2,1)S(1)}, bf16[128]{0:T(256)(128)(2,1)}, u32[]{:S(2)}) copy-start(bf16[128]{0:T(256)(128)(2,1)} %param.19) | copy-start | bytes 772

commit v7 on v6

--- a/solution.py
+++ b/solution.py
@@ -43,7 +43,7 @@
 
 def kernel(
     owner_hbm, item_hbm, seg_hbm, nbr_hbm, gain_hbm, table_hbm, w_hbm, wo_hbm, wctx_hbm,
-    states, counts, wctx,
+    states, counts, wctx, scored,
     owner_ref, item_ref, seg_ref, nbr_ref, gain_ref,
     tcol, w4, wp, wo, gbuf, reqout, reqin, repout, repin, pick, part0, partin, xcols,
     mask, nrm, feats, part, rsin, xrow,
@@ -323,8 +323,11 @@
                 states[h, m] = new
                 to_group(lambda to: states.at[h, m], states.at[h, m], ag_s.at[2], ag_r.at[2, h])
 
-    for h in range(2):
-        drain(states.at[h, pl.ds(0, MP - 1)], ag_r.at[2, h])
+    drain(states.at[0, pl.ds(0, MP - 1)], ag_r.at[2, 0])
+    scored[...] = jnp.dot(
+        states[0].reshape(HALF, D), wctx[...], preferred_element_type=F32
+    ).astype(BF16)
+    drain(states.at[1, pl.ds(0, MP - 1)], ag_r.at[2, 1])
 
     for copy in exchange:
         copy.wait_send()
@@ -349,15 +352,24 @@
             drain(part.at[sec, h, pl.ds(0, MP - 1)], rs_s.at[sec])
 
 
-def finish(states_ref, counts_ref, wctx_ref, bias_ref, out_hbm, ctx_ref, sem):
-    write = pltpu.make_async_copy(states_ref, out_hbm, sem)
-    write.start()
-    scored = jnp.dot(
-        states_ref[...].reshape(ROWS, D), wctx_ref[...], preferred_element_type=F32
+def finish(
+    states_ref, counts_ref, wctx_ref, scored_ref, bias_ref, out_hbm, ctx_hbm, ctx_ref, sem
+):
+    writes = [
+        pltpu.make_async_copy(states_ref.at[h], out_hbm.at[h], sem.at[h]) for h in range(2)
+    ]
+    for write in writes:
+        write.start()
+    rest = jnp.dot(
+        states_ref[1].reshape(HALF, D), wctx_ref[...], preferred_element_type=F32
     ).astype(BF16)
-    summed = jnp.dot(counts_ref[...], scored, preferred_element_type=F32)
+    summed = jnp.dot(counts_ref[:, :HALF], scored_ref[...], preferred_element_type=F32)
+    summed = summed + jnp.dot(counts_ref[:, HALF:], rest, preferred_element_type=F32)
     ctx_ref[...] = silu(summed + bias_ref[...].astype(F32)).astype(BF16)
-    write.wait()
+    writes.append(pltpu.make_async_copy(ctx_ref, ctx_hbm, sem.at[2]))
+    writes[2].start()
+    for write in writes:
+        write.wait()
 
 
 def on_device(
@@ -367,15 +379,16 @@
     vmem = pl.BlockSpec(memory_space=pltpu.VMEM)
     hbm = pl.BlockSpec(memory_space=pltpu.HBM)
     dma = pltpu.SemaphoreType.DMA
-    states, counts, wctx = pl.pallas_call(
+    states, counts, wctx, scored = pl.pallas_call(
         kernel,
         out_shape=(
             pltpu.VMEM((2, MP, OWN, D), BF16),
             pltpu.VMEM((ROWS, ROWS), BF16),
             pltpu.VMEM((D, HD), BF16),
+            pltpu.VMEM((HALF, HD), BF16),
         ),
         in_specs=[hbm] * 9,
-        out_specs=(vmem, vmem, vmem),
+        out_specs=(vmem, vmem, vmem, vmem),
         scratch_shapes=[
             pltpu.VMEM((1, n_rows), I32),
             pltpu.VMEM((1, n_rows), I32),
@@ -436,12 +449,12 @@
             jax.ShapeDtypeStruct((2, MP, OWN, D), BF16),
             jax.ShapeDtypeStruct((ROWS, HD), BF16),
         ),
-        in_specs=[vmem] * 4,
-        out_specs=(hbm, vmem),
-        scratch_shapes=[dma(())],
+        in_specs=[vmem] * 5,
+        out_specs=(hbm, hbm),
+        scratch_shapes=[pltpu.VMEM((ROWS, HD), BF16), dma((3,))],
         compiler_params=pltpu.CompilerParams(vmem_limit_bytes=8 * 1024 * 1024),
         name="finish",
-    )(states, counts, wctx, ctx_bias.reshape(1, -1))
+    )(states, counts, wctx, scored, ctx_bias.reshape(1, -1))
     return states.reshape(1, 1, ROWS, D), ctx.reshape(1, 1, ROWS, HD)
 
 

time: 73.4 us -> 73 us (level)
  no operation moved by 1% of the time
where the time goes in v7:
time: 73 us; the launch traced here: 72.2 us
  Pallas kernels  71.5 us (98%)
    pallas_call x1, Pallas kernels, on_device(): pl.pallas_call(kernel, out_shape=(pltpu.VMEM((2, MP, OWN, D), BF16), pltp...  70.4 us

profile of v7, /device:TPU:1, one launch (start us, length us, event | category | flops | bytes accessed | tf_op | source)
XLA Modules:
  0.0 72.2 jit_solution(18146926966327202510)
XLA Ops:
  0.6 0.0 copy-start
  0.6 70.4 %cascade.1 = (bf16[2,8,16,1024]{3,2,1,0:T(8,128)(2,1)S(1)}, bf16[256,256]{1,0:T(8,128)(2,1)S(1)}, bf16[1024,128]{1,0:T(8,128)(2,1)S(1)}, bf16[128,128]{1,0:T(8,128)(2,1)S(1)}) custom-call(s32[1,512]{1,0:T(1,128)} %bitcast.15, s32[1,512]{1,0:T(1,128)} %bitcast.16, s32[2,256]{1,0:T(2,128)} %bitcast.17, s32[2,8,256]{2,1,0:T(8,128)} %bitcast.14, ...), custom_call_target="tpu_custom_call" | custom-call | tf_op jit(solution)/shard_map/cascade/pallas_call | solution.py:382
  71.1 0.0 copy-done
  71.1 1.1 %finish.1 = (bf16[2,8,16,1024]{3,2,1,0:T(8,128)(2,1)}, bf16[256,128]{1,0:T(8,128)(2,1)}) custom-call(bf16[2,8,16,1024]{3,2,1,0:T(8,128)(2,1)S(1)} %get-tuple-element.8.states_ref, bf16[256,256]{1,0:T(8,128)(2,1)S(1)} %get-tuple-element.9.counts_ref, bf16[1024,128]{1,0:T(8,128)(2,1)S(1)} %get-tuple-element.10.wctx_ref, ...), custom_call_target="tpu_custom_call" | custom-call | tf_op jit(solution)/shard_map/finish/pallas_call | solution.py:446
Async XLA Ops:
  0.6 70.5 %copy-start = (bf16[128]{0:T(256)(128)(2,1)S(1)}, bf16[128]{0:T(256)(128)(2,1)}, u32[]{:S(2)}) copy-start(bf16[128]{0:T(256)(128)(2,1)} %param.19) | copy-start | bytes 772

commit v8 on v7

--- a/solution.py
+++ b/solution.py
@@ -47,7 +47,7 @@
     owner_ref, item_ref, seg_ref, nbr_ref, gain_ref,
     tcol, w4, wp, wo, gbuf, reqout, reqin, repout, repin, pick, part0, partin, xcols,
     mask, nrm, feats, part, rsin, xrow,
-    loc, req_s, req_r, rep_s, rep_r, wex_s, wex_r, xp_s, xp_r, ag_s, ag_r, rs_s, rs_r,
+    loc, req_s, req_r, rep_s, rep_r, wex_s, wex_r, xp_s, xp_r, ag_s, ag_r, rs_s, rs_r, fin_r,
 ):
     g = lax.axis_index("dp")
     m = lax.axis_index("mp")
@@ -271,6 +271,14 @@
         swaps[h].wait_recv()
         xcols[h, m] = mine[h] + partin[h]
         to_group(lambda to: xcols.at[h, m], xcols.at[h, m], ag_s.at[0], ag_r.at[0, h])
+
+    row_start = m - m % 4
+    m_across = row_start + lax.rem(m + 2, 4)
+    m_beside = (row_start + lax.rem(m + 1, 4), row_start + lax.rem(m + 3, 4))
+
+    def pass_states(src, to):
+        rows_of = states.at[0, src]
+        remote(rows_of, rows_of, ag_s.at[2], fin_r.at[src], (g, to, p)).start()
 
     own_row = pl.multiple_of(m * OWN, OWN)
     for sec in range(2):
@@ -321,9 +329,22 @@
                 to_group(lambda to: nrm.at[1, h, m], nrm.at[1, h, m], ag_s.at[1], ag_r.at[1, h])
             else:
                 states[h, m] = new
-                to_group(lambda to: states.at[h, m], states.at[h, m], ag_s.at[2], ag_r.at[2, h])
-
-    drain(states.at[0, pl.ds(0, MP - 1)], ag_r.at[2, 0])
+                if h == 1:
+                    to_group(lambda to: states.at[1, m], states.at[1, m], ag_s.at[2], ag_r.at[2, 1])
+                else:
+                    for to in (m_across, m_y) + m_beside:
+                        pass_states(m, to)
+
+    drain(states.at[0, m_y], fin_r.at[m_y])
+    for to in m_beside:
+        pass_states(m_y, to)
+    drain(states.at[0, m_across], fin_r.at[m_across])
+    pass_states(m_across, m_y)
+    for src in m_beside:
+        drain(states.at[0, src], fin_r.at[src])
+    for src in m_beside + (m_across,):
+        turned = lax.rem(src + MP // 2, MP)
+        drain(states.at[0, turned], fin_r.at[turned])
     scored[...] = jnp.dot(
         states[0].reshape(HALF, D), wctx[...], preferred_element_type=F32
     ).astype(BF16)
@@ -427,6 +448,7 @@
             dma((3, 2)),
             dma((2,)),
             dma((2, 2, MP)),
+            dma((MP,)),
         ],
         compiler_params=pltpu.CompilerParams(
             collective_id=0, has_side_effects=True, vmem_limit_bytes=65700000

time: 73 us -> 72.7 us (level)
  no operation moved by 1% of the time
where the time goes in v8:
time: 72.7 us; the launch traced here: 72.1 us
  Pallas kernels  71.4 us (98%)
    pallas_call x1, Pallas kernels, on_device(): pl.pallas_call(kernel, out_shape=(pltpu.VMEM((2, MP, OWN, D), BF16), pltp...  70.3 us

profile of v8, /device:TPU:1, one launch (start us, length us, event | category | flops | bytes accessed | tf_op | source)
XLA Modules:
  0.0 72.1 jit_solution(16756879620994935010)
XLA Ops:
  0.6 0.0 copy-start
  0.6 70.3 %cascade.1 = (bf16[2,8,16,1024]{3,2,1,0:T(8,128)(2,1)S(1)}, bf16[256,256]{1,0:T(8,128)(2,1)S(1)}, bf16[1024,128]{1,0:T(8,128)(2,1)S(1)}, bf16[128,128]{1,0:T(8,128)(2,1)S(1)}) custom-call(s32[1,512]{1,0:T(1,128)} %bitcast.15, s32[1,512]{1,0:T(1,128)} %bitcast.16, s32[2,256]{1,0:T(2,128)} %bitcast.17, s32[2,8,256]{2,1,0:T(8,128)} %bitcast.14, ...), custom_call_target="tpu_custom_call" | custom-call | tf_op jit(solution)/shard_map/cascade/pallas_call | solution.py:403
  71.0 0.0 copy-done
  71.0 1.1 %finish.1 = (bf16[2,8,16,1024]{3,2,1,0:T(8,128)(2,1)}, bf16[256,128]{1,0:T(8,128)(2,1)}) custom-call(bf16[2,8,16,1024]{3,2,1,0:T(8,128)(2,1)S(1)} %get-tuple-element.8.states_ref, bf16[256,256]{1,0:T(8,128)(2,1)S(1)} %get-tuple-element.9.counts_ref, bf16[1024,128]{1,0:T(8,128)(2,1)S(1)} %get-tuple-element.10.wctx_ref, ...), custom_call_target="tpu_custom_call" | custom-call | tf_op jit(solution)/shard_map/finish/pallas_call | solution.py:468
Async XLA Ops:
  0.6 70.4 %copy-start = (bf16[128]{0:T(256)(128)(2,1)S(1)}, bf16[128]{0:T(256)(128)(2,1)}, u32[]{:S(2)}) copy-start(bf16[128]{0:T(256)(128)(2,1)} %param.19) | copy-start | bytes 772
